TPU v7x, 256 devices: a whole 4x4x8 slice. The times are simulated.
256 devices in a mesh: row: 16 (over z, core), col: 16 (over x, y).
Axes of the slice: x: 4, y: 4, z: 8, core: 2. Of those that a mesh axis runs over, the one named last changes fastest.
Arguments:
- child_samples: bfloat16 [2, 2, 256, 262144], P(None, None, 'col', 'row'), may hold values from -6 to 6
- child_map: int32 [2, 2048], P(None, 'row'), may hold values from 0 to 127, as said below
- forward_probe: bfloat16 [256, 262144], P(None, ('row', 'col')), may hold values from -6 to 6
- adjoint_probe: bfloat16 [256, 262144], P(None, ('row', 'col')), may hold values from -6 to 6
- stored_sparse_blocks: bfloat16 [2048, 18, 128, 128], P(('row', 'col')), may hold values from -0.125 to 0.125
- block_pattern: int32 [16, 128, 18], P(None, 'col'), may hold values from 0 to 7
Outputs:
- row_basis: bfloat16 [256, 262144], P(None, ('row', 'col'))
- column_basis: bfloat16 [256, 262144], P(None, ('row', 'col'))
- transfers: float32 [2, 2, 65536, 256], P(None, None, ('row', 'col'))
Inputs may be any that keep to these rules, and one draw needn't show every extreme that they name: Within each aligned group of 16 * 8 front blocks (one row group), each row of child_map is a permutation of 0 to 16 * 8 - 1.
All inputs are finite; a program needn't handle non-finite values.
Results may differ from a plain program's by a relative error of at most 0.0055.
Values may be sent and summed in bfloat16 or wider, within the bound.
A program may use at most 128 MiB of HBM per device.

v0:
```python
from functools import partial
import math

import jax
import jax.numpy as jnp
from jax import lax
from jax.sharding import PartitionSpec as P

S = 256
BLK = 128
SLOTS = 6


def padded(x, sides, width):
    for axis, dim in sides:
        peers, length = (lax.axis_size(axis), x.shape[dim])
        up = [(i, (i + 1) % peers) for i in range(peers - 1)]
        down = [(j, i) for i, j in up]
        last = lax.slice_in_dim(x, length - width, length, axis=dim)
        leading = lax.slice_in_dim(x, 0, width, axis=dim)
        before = lax.ppermute(last, axis, up)
        after = lax.ppermute(leading, axis, down)
        x = jnp.concatenate([before, x, after], axis=dim)
    return x


def shifted(block, axis, distance):
    devices = range(lax.axis_size(axis))
    route = [(i - distance, i) for i in devices if i - distance in devices]
    return lax.ppermute(block, axis, route)


def from_partner(value, axis, bit):
    mask = 2**bit
    pairs = [(source, source ^ mask) for source in range(lax.axis_size(axis))]
    return lax.ppermute(value, axis, pairs)


def spread_terms(targets, sketch_products, width):
    onehot = (targets[..., None] == jnp.arange(width, dtype=jnp.int32)).astype(jnp.float32)
    return jnp.einsum("bkg,bksc->sgc", onehot, sketch_products, precision=lax.Precision.HIGHEST)


def local(
    child_samples, child_map, forward_probe, adjoint_probe, stored_sparse_blocks, block_pattern
):
    samples_here = child_samples.shape[2]
    rows_group = child_samples.shape[3]
    group_blocks = rows_group // BLK
    leaf_rows = forward_probe.shape[1]
    leaf_blocks = leaf_rows // BLK
    row_pos = lax.axis_index("row")
    blocked = child_samples.reshape(2, 2, samples_here, group_blocks, BLK)
    first_child = jnp.take(blocked[0], child_map[0], axis=2).astype(jnp.float32)
    second_child = jnp.take(blocked[1], child_map[1], axis=2).astype(jnp.float32)
    extended = (
        (first_child + second_child).astype(jnp.bfloat16).reshape(2, samples_here, rows_group)
    )
    regrouped = lax.all_to_all(extended, "col", split_axis=2, concat_axis=1, tiled=True)
    own_pattern = lax.dynamic_index_in_dim(block_pattern, row_pos, 0, keepdims=False)
    regions = jnp.arange(3 * SLOTS, dtype=jnp.int32) // SLOTS
    flat_index = regions[None, :] * leaf_blocks + own_pattern
    probe_ext = padded(forward_probe, (("row", 1),), leaf_rows)
    conjugate_transpose_rows = adjoint_probe.reshape(S, leaf_blocks, BLK)
    sketch_products = jnp.einsum(
        "mda,duai->dumi",
        conjugate_transpose_rows,
        stored_sparse_blocks,
        preferred_element_type=jnp.float32,
    )
    terms = spread_terms(flat_index, sketch_products, 3 * leaf_blocks).reshape(S, 3, leaf_rows)
    from_above = shifted(terms[:, 0].astype(jnp.bfloat16), "row", -1).astype(jnp.float32)
    from_below = shifted(terms[:, 2].astype(jnp.bfloat16), "row", 1).astype(jnp.float32)
    adjoint_sparse = terms[:, 1] + from_above + from_below
    probe_blocks = probe_ext.reshape(S, 3 * leaf_blocks, BLK)
    selector = (flat_index[..., None] == jnp.arange(3 * leaf_blocks, dtype=jnp.int32)).astype(
        jnp.bfloat16
    )
    collected_samples = jnp.einsum(
        "jhc,wct->wjht", selector, probe_blocks, preferred_element_type=jnp.float32
    ).astype(jnp.bfloat16)
    forward_sparse = jnp.einsum(
        "wjht,jhot->wjo",
        collected_samples,
        stored_sparse_blocks,
        preferred_element_type=jnp.float32,
    ).reshape(S, leaf_rows)
    samples = jnp.stack(
        [
            regrouped[0].astype(jnp.float32) + forward_sparse,
            regrouped[1].astype(jnp.float32) + adjoint_sparse,
        ]
    )
    grams = jnp.einsum("ksr,ktr->kst", samples, samples, precision=lax.Precision.HIGHEST)
    level_one = grams + from_partner(grams.astype(jnp.bfloat16), "col", 0).astype(grams.dtype)
    level_two = level_one + from_partner(level_one.astype(jnp.bfloat16), "col", 1).astype(
        level_one.dtype
    )
    stacked_grams = jnp.concatenate([grams, level_one, level_two], axis=0)
    factors = jnp.linalg.cholesky(stacked_grams)
    identity = jnp.broadcast_to(jnp.eye(S, dtype=jnp.float32), factors.shape)
    inverses = jax.vmap(partial(jax.scipy.linalg.solve_triangular, lower=True))(factors, identity)
    factor_leaf = factors[0:2]
    factor_one = factors[2:4]
    inverse_leaf = inverses[0:2]
    inverse_one = inverses[2:4]
    inverse_two = inverses[4:6]
    bases = (
        jnp.einsum("kst,ktr->ksr", inverse_leaf, samples, precision=lax.Precision.HIGHEST)
        * math.sqrt(leaf_rows)
    ).astype(jnp.bfloat16)
    first = jnp.einsum("kst,ktu->kus", inverse_one, factor_leaf, precision=lax.Precision.HIGHEST)
    second = jnp.einsum("kst,ktu->kus", inverse_two, factor_one, precision=lax.Precision.HIGHEST)
    transfers = jnp.stack([first, second], axis=1)
    return (bases[0], bases[1], transfers)


def solution(mesh):
    return jax.shard_map(
        local,
        mesh=mesh,
        in_specs=(
            P(None, None, "col", "row"),
            P(None, "row"),
            P(None, ("row", "col")),
            P(None, ("row", "col")),
            P(("row", "col"), None, None, None),
            P(None, "col", None),
        ),
        out_specs=(
            P(None, ("row", "col")),
            P(None, ("row", "col")),
            P(None, None, ("row", "col"), None),
        ),
        check_vma=False,
    )
```

profile of v0, /device:TPU:96, one launch (start us, length us, event | category | flops | bytes accessed | tf_op | source)
XLA Modules:
  0.0 524.2 jit_solution(15192901601436697136)
XLA Ops:
  2.6 2.4 collective-permute-start
  12.9 12.7 %copy.136 = bf16[2,16,128,128]{1,0,3,2:T(2,128)(2,1)} copy(bf16[2,16,128,128]{3,1,0,2:T(8,128)(2,1)S(1)} %add_convert_fusion) | data formatting | bytes 2097152 | tf_op jit(solution)/shard_map/reshape | solution.py:57
  25.6 11.2 %reshape.174 = bf16[16,2,16384]{2,1,0:T(2,128)(2,1)} reshape(bf16[16384,2,16]{2,1,0:T(2,128)(2,1)} %bitcast.127) | data formatting | bytes 2097152
  36.8 7.2 %all-to-all-start = ((bf16[16,2,16384]{2,1,0:T(2,128)(2,1)}), bf16[16,2,16384]{2,1,0:T(2,128)(2,1)}, u32[]{:S(2)}, u32[]{:S(2)}) async-start(bf16[16,2,16384]{2,1,0:T(2,128)(2,1)} %reshape.174), calls=%async_computation | async-start | bytes 2097152 | tf_op jit(solution)/shard_map/all_to_all | solution.py:59
  44.2 11.5 %convolution_bitcast_fusion = f32[8,18,256,128]{2,3,1,0:T(8,128)} fusion(bf16[8,18,128,128]{3,2,1,0:T(8,128)(2,1)} %param.12, bf16[256,8,128,1]{2,1,0,3:T(8,128)(2,1)S(1)} %bitcast.136), kind=kOutput, calls=%fused_computation.7 | convolution fusion | flops 1207959552 | bytes 24117248 | tf_op jit(solution)/shard_map/mda,duai->dumi/dot_general | solution.py:65
  55.7 22.1 %copy.108 = f32[8,18,256,128]{3,1,0,2:T(8,128)} copy(f32[8,18,256,128]{2,3,1,0:T(8,128)} %convolution_bitcast_fusion) | data formatting | bytes 37748736 | tf_op jit(solution)/shard_map/mda,duai->dumi/transpose | solution.py:65
  78.5 12.8 %convolution_bitcast_fusion.1 = f32[256,24,128]{2,1,0:T(8,128)S(1)} fusion(f32[8,18,256,128]{3,1,0,2:T(8,128)} %copy.108, s32[8,18]{1,0:T(8,128)S(1)} %bitcast_add_fusion.2), kind=kOutput, calls=%fused_computation.11 | convolution fusion | flops 1358957952 | bytes 22020672 | tf_op jit(solution)/shard_map/bkg,bksc->sgc/dot_general | solution.py:41
  91.3 2.4 copy.109
  93.7 2.4 copy.110
  97.4 4.4 collective-permute-start.3
  106.2 6.4 %convert_bitcast_fusion = bf16[256,8,18,128]{3,2,1,0:T(8,128)(2,1)} fusion(bf16[256,24,128,1]{2,1,0,3:T(8,128)(2,1)S(1)} %bitcast.130, s32[8,18]{1,0:T(8,128)S(1)} %bitcast_add_fusion.2), kind=kOutput, calls=%fused_computation.4 | convolution fusion | flops 231214464 | bytes 11010624 | tf_op jit(solution)/shard_map/jhc,wct->wjht/dot_general | solution.py:79
  112.6 12.4 %fusion = f32[8,256,128,1]{1,2,3,0:T(8,128)} fusion(bf16[8,18,128,128]{3,2,1,0:T(8,128)(2,1)} %param.12, bf16[256,8,18,128]{3,2,1,0:T(8,128)(2,1)} %convert_bitcast_fusion), kind=kOutput, calls=%fused_computation.5 | convolution fusion | flops 1207959552 | bytes 15204352 | tf_op jit(solution)/shard_map/wjht,jhot->wjo/dot_general | solution.py:82
  125.0 2.6 copy.104
  127.7 8.9 %reshape.175 = bf16[16384,2,16]{2,1,0:T(2,128)(2,1)} reshape(bf16[16,2,16384]{2,1,0:T(2,128)(2,1)} %all-to-all-done) | data formatting | bytes 2097152
  136.6 12.7 %copy.137 = bf16[2,16,16,1024]{3,2,1,0:T(8,128)(2,1)} copy(bf16[2,16,16,1024]{1,0,3,2:T(2,128)(2,1)} %bitcast.128) | data formatting | bytes 2097152 | tf_op jit(solution)/shard_map/all_to_all | solution.py:59
  154.6 2.3 fusion.57
  159.2 6.8 %collective-permute-done.4 = bf16[2,256,256]{1,2,0:T(8,128)(2,1)S(1)} collective-permute-done((bf16[2,256,256]{1,2,0:T(8,128)(2,1)S(1)}, bf16[2,256,256]{1,2,0:T(8,128)(2,1)S(1)}, u32[]{:S(2)}, u32[]{:S(2)}) %collective-permute-start.4) | collective-permute-done | bytes 262176 | tf_op jit(solution)/shard_map/ppermute | solution.py:36
  166.1 3.2 collective-permute-start.5
  170.6 5.4 %collective-permute-done.5 = bf16[2,256,256]{1,2,0:T(8,128)(2,1)S(1)} collective-permute-done((bf16[2,256,256]{1,2,0:T(8,128)(2,1)S(1)}, bf16[2,256,256]{1,2,0:T(8,128)(2,1)S(1)}, u32[]{:S(2)}, u32[]{:S(2)}) %collective-permute-start.5) | collective-permute-done | bytes 262176 | tf_op jit(solution)/shard_map/ppermute | solution.py:36
  180.4 70.5 %custom-call.17 = f32[6,128,128]{2,1,0:T(8,128)S(1)} custom-call(f32[6,128,128]{2,1,0:T(8,128)S(1)} %cholesky.122), custom_call_target="Cholesky" | custom-call | tf_op jit(solution)/shard_map/jit(cholesky)/cholesky | solution.py:100
  252.5 60.4 %custom-call.18 = f32[6,1,128,128]{2,3,1,0:T(8,128)} custom-call(f32[6,1,128,128]{3,2,1,0:T(8,128)} %select_bitcast_fusion), custom_call_target="InvertDiagBlocksLowerTriangular" | custom-call | tf_op jit(solution)/shard_map/jit(cholesky)/cholesky | solution.py:100
  316.1 71.1 %custom-call.19 = f32[6,128,128]{2,1,0:T(8,128)S(1)} custom-call(f32[6,128,128]{2,1,0:T(8,128)} %slice_subtract_fusion), custom_call_target="Cholesky" | custom-call | tf_op jit(solution)/shard_map/jit(cholesky)/cholesky | solution.py:100
  388.8 5.6 %while.1 = (s32[]{:T(128)}, f32[6,256,256]{2,1,0:T(8,128)S(1)}, s32[2,2]{1,0:T(2,128)S(1)}, f32[2,6,128,128]{3,2,0,1:T(8,128)}, s32[]{:T(128)}) while((s32[]{:T(128)}, f32[6,256,256]{2,1,0:T(8,128)S(1)}, s32[2,2]{1,0:T(2,128)S(1)}, f32[2,6,128,128]{3,2,0,1:T(8,128)}, s32[]{:T(128)}) %tuple.44), condition=%wide.while_cond, body=%wide.while_body.sunk | while | flops 2 | bytes 787565 | solution.py:102
  394.4 119.5 %custom-call.20 = f32[6,2,128,128]{2,3,1,0:T(8,128)} custom-call(f32[6,2,128,128]{3,2,1,0:T(8,128)} %bitcast.139), custom_call_target="InvertDiagBlocksLowerTriangular" | custom-call | tf_op jit(solution)/shard_map/vmap(jit(_solve_triangular))/triangular_solve | solution.py:102
  (96 shorter events, 51.5 us)
Async XLA Ops:
  0.6 104.0 %collective-permute-start.1 = (bf16[256,1024]{1,0:T(8,128)(2,1)}, bf16[256,1024]{1,0:T(8,128)(2,1)}, u32[]{:S(2)}, u32[]{:S(2)}) collective-permute-start(bf16[256,1024]{1,0:T(8,128)(2,1)} %param.10), channel_id=1, source_target_pairs={{16,0},{32,16},{48,32},{64,48},{80,64},{96,80},{112,96},{128,112},... | collective-permute-start | bytes 1572872 | tf_op jit(solution)/shard_map/ppermute | solution.py:22
  2.6 102.1 %collective-permute-start = (bf16[256,1024]{1,0:T(8,128)(2,1)}, bf16[256,1024]{1,0:T(8,128)(2,1)}, u32[]{:S(2)}, u32[]{:S(2)}) collective-permute-start(bf16[256,1024]{1,0:T(8,128)(2,1)} %param.10), channel_id=1, source_target_pairs={{0,16},{16,32},{32,48},{48,64},{64,80},{80,96},{96,112},{112,128},... | collective-permute-start | bytes 1572872 | tf_op jit(solution)/shard_map/ppermute | solution.py:21
  6.9 0.7 copy-start.12
  36.8 7.2 %copy-start.8 = (bf16[256,1024]{1,0:T(8,128)(2,1)S(1)}, bf16[256,1024]{1,0:T(8,128)(2,1)}, u32[]{:S(2)}) copy-start(bf16[256,1024]{1,0:T(8,128)(2,1)} %param.11) | copy-start | bytes 1572868
  36.8 90.8 %all-to-all-start = ((bf16[16,2,16384]{2,1,0:T(2,128)(2,1)}), bf16[16,2,16384]{2,1,0:T(2,128)(2,1)}, u32[]{:S(2)}, u32[]{:S(2)}) async-start(bf16[16,2,16384]{2,1,0:T(2,128)(2,1)} %reshape.174), calls=%async_computation | async-start | bytes 2097152 | tf_op jit(solution)/shard_map/all_to_all | solution.py:59
  96.3 8.3 %copy-start.11 = (bf16[256,1024]{1,0:T(8,128)(2,1)S(1)}, bf16[256,1024]{1,0:T(8,128)(2,1)}, u32[]{:S(2)}) copy-start(bf16[256,1024]{1,0:T(8,128)(2,1)} %param.10) | copy-start | bytes 1572868
  97.4 55.4 %collective-permute-start.3 = (bf16[256,1024]{1,0:T(8,128)(2,1)}, bf16[256,1024]{1,0:T(8,128)(2,1)}, u32[]{:S(2)}, u32[]{:S(2)}) collective-permute-start(bf16[256,1024]{1,0:T(8,128)(2,1)} %get-tuple-element.48), channel_id=1, source_target_pairs={{0,16},{16,32},{32,48},{48,64},{64,80},{80,96},{96,112},{112,128},... | collective-permute-start | bytes 1572872 | tf_op jit(solution)/shard_map/ppermute | solution.py:30
  101.7 51.0 %collective-permute-start.2 = (bf16[256,1024]{1,0:T(8,128)(2,1)}, bf16[256,1024]{1,0:T(8,128)(2,1)}, u32[]{:S(2)}, u32[]{:S(2)}) collective-permute-start(bf16[256,1024]{1,0:T(8,128)(2,1)} %get-tuple-element.47), channel_id=1, source_target_pairs={{16,0},{32,16},{48,32},{64,48},{80,64},{96,80},{112,96},{128,112},... | collective-permute-start | bytes 1572872 | tf_op jit(solution)/shard_map/ppermute | solution.py:30
  151.3 1.2 copy-start.5
  152.7 1.8 copy-start
  154.6 4.7 copy-start.2
  156.9 9.2 %collective-permute-start.4 = (bf16[2,256,256]{1,2,0:T(8,128)(2,1)S(1)}, bf16[2,256,256]{1,2,0:T(8,128)(2,1)S(1)}, u32[]{:S(2)}, u32[]{:S(2)}) collective-permute-start(bf16[2,256,256]{1,2,0:T(8,128)(2,1)S(1)} %get-tuple-element.58), channel_id=1, source_target_pairs={{0,1},{1,0},{2,3},{3,2},{4,5},{5,4},{6,7},{7,6},{8,9},{9,8},{10,11... | collective-permute-start | bytes 786440 | tf_op jit(solution)/shard_map/ppermute | solution.py:36
  166.1 9.9 %collective-permute-start.5 = (bf16[2,256,256]{1,2,0:T(8,128)(2,1)S(1)}, bf16[2,256,256]{1,2,0:T(8,128)(2,1)S(1)}, u32[]{:S(2)}, u32[]{:S(2)}) collective-permute-start(bf16[2,256,256]{1,2,0:T(8,128)(2,1)S(1)} %get-tuple-element.37), channel_id=1, source_target_pairs={{0,2},{1,3},{2,0},{3,1},{4,6},{5,7},{6,4},{7,5},{8,10},{9,11},{10,... | collective-permute-start | bytes 786440 | tf_op jit(solution)/shard_map/ppermute | solution.py:36
  176.1 0.8 copy-start.4
  387.6 1.1 copy-start.13
  388.8 125.2 %copy-start.10 = (f32[128,256]{1,0:T(8,128)S(1)}, f32[128,256]{1,0:T(8,128)}, u32[]{:S(2)}) copy-start(f32[128,256]{1,0:T(8,128)} %get-tuple-element.55) | copy-start | bytes 393220
  388.8 127.1 %copy-start.9 = (f32[128,256]{1,0:T(8,128)S(1)}, f32[128,256]{1,0:T(8,128)}, u32[]{:S(2)}) copy-start(f32[128,256]{1,0:T(8,128)} %get-tuple-element.54) | copy-start | bytes 393220
  513.9 2.8 copy-start.7
  515.9 1.7 copy-start.1
  515.9 1.7 copy-start.3
  517.6 2.0 copy-start.6
where the time goes:
time: 535 us; the launch traced here: 524 us
  other arithmetic  336 us (63%)
  local copies, waits for them, and re-layouts  95.4 us (18%)
  matrix products  56.3 us (11%)
  starting transfers between devices  23 us (4%)
  waiting for transfers between devices  12.3 us (2%)
    another operation x10, other arithmetic, local(): factors = jnp.linalg.cholesky(stacked_grams)  204 us
    another operation x4, other arithmetic, local(): jax.vmap(partial(jax.scipy.linalg.solve_triangular, lower=True))  122 us
    unnamed x35, local copies, waits for them, and re-layouts  23.5 us
    transpose x1, local copies, waits for them, and re-layouts, local(): jnp.einsum('mda,duai->dumi', conjugate_transpose_rows, stored_sparse_bloc...  22.1 us
    dot_general x1, matrix products, spread_terms(): jnp.einsum('bkg,bksc->sgc', onehot, sketch_products, precision=lax.Precis...  12.8 us
    reshape x1, local copies, waits for them, and re-layouts, local(): (first_child + second_child).astype(jnp.bfloat16)  12.7 us
    all_to_all x1, local copies, waits for them, and re-layouts, local(): lax.all_to_all(extended, 'col', split_axis=2, concat_axis=1, tiled=True)  12.7 us
    dot_general x1, matrix products, local(): jnp.einsum('wjht,jhot->wjo', collected_samples, stored_sparse_blocks, pre...  12.4 us
  transfers between devices with their start and end apart: 7, of which 2 were waited for; matrix products, arithmetic and copies ran while one was open for 26% of the time, Pallas kernels for 0%

commit v1 on v0

v1 whole, which is shorter than its diff:
```python
import math

import jax
import jax.numpy as jnp
from jax import lax
from jax.experimental import pallas as pl
from jax.experimental.pallas import tpu as pltpu
from jax.sharding import PartitionSpec as P

S = 256
BLK = 128
SLOTS = 6
PANEL = 32
PITCH = S + 8
F32 = jnp.float32
BF16 = jnp.bfloat16
HIGHEST = lax.Precision.HIGHEST
VMEM_LIMIT = 56 << 20


def params():
    return pltpu.CompilerParams(vmem_limit_bytes=VMEM_LIMIT)


def split3(x):
    high = x.astype(BF16)
    rest = x - high.astype(F32)
    mid = rest.astype(BF16)
    low = (rest - mid.astype(F32)).astype(BF16)
    return high, mid, low


def dot3(a, b, dims):
    ah, am, _ = split3(a)
    bh, bm, _ = split3(b)
    dn = (dims, ((), ()))
    out = lax.dot_general(ah, bh, dn, preferred_element_type=F32)
    out += lax.dot_general(ah, bm, dn, preferred_element_type=F32)
    out += lax.dot_general(am, bh, dn, preferred_element_type=F32)
    return out


def extend_kernel(map_ref, child_ref, out_ref):
    leaves = out_ref.shape[0]
    blocks = out_ref.shape[3] // BLK

    def leaf(d, carry):
        for b in range(blocks):
            first = pl.multiple_of(map_ref[0, d * blocks + b] * BLK, BLK)
            second = pl.multiple_of(map_ref[1, d * blocks + b] * BLK, BLK)
            for k in range(2):
                x = child_ref[0, k, :, pl.ds(first, BLK)].astype(F32)
                y = child_ref[1, k, :, pl.ds(second, BLK)].astype(F32)
                out_ref[d, k, :, b * BLK : (b + 1) * BLK] = (x + y).astype(BF16)
        return carry

    lax.fori_loop(0, leaves, leaf, 0)


def extend(child_map, child_samples, leaves):
    samples_here, rows_group = child_samples.shape[2:]
    return pl.pallas_call(
        extend_kernel,
        out_shape=jax.ShapeDtypeStruct((leaves, 2, samples_here, rows_group // leaves), BF16),
        in_specs=[
            pl.BlockSpec(memory_space=pltpu.SMEM),
            pl.BlockSpec(memory_space=pltpu.VMEM),
        ],
        out_specs=pl.BlockSpec(memory_space=pltpu.VMEM),
        compiler_params=params(),
        cost_estimate=pl.CostEstimate(flops=1 << 20, bytes_accessed=3 << 20, transcendentals=0),
        name="extend",
    )(child_map, child_samples)


def adjoint_kernel(pattern_ref, probe_ref, sparse_ref, above_ref, own_ref, below_ref, acc):
    b = pl.program_id(0)

    @pl.when(b == 0)
    def _():
        acc[...] = jnp.zeros_like(acc)

    probe = probe_ref[...]
    for s in range(0, 3 * SLOTS, 2):
        pair = jnp.concatenate([sparse_ref[0, s], sparse_ref[0, s + 1]], axis=1)
        product = jnp.dot(probe, pair, preferred_element_type=F32)
        for i in range(2):
            target = pattern_ref[b, s + i]
            acc[s // SLOTS, target] += product[:, i * BLK : (i + 1) * BLK]

    @pl.when(b == pl.num_programs(0) - 1)
    def _():
        above_ref[...] = acc[0].astype(BF16)
        own_ref[...] = acc[1]
        below_ref[...] = acc[2].astype(BF16)


def adjoint(pattern, probe, sparse):
    blocks = sparse.shape[0]
    shape = (blocks, S, BLK)
    whole = pl.BlockSpec(shape, lambda b: (0, 0, 0))
    return pl.pallas_call(
        adjoint_kernel,
        grid=(blocks,),
        out_shape=[
            jax.ShapeDtypeStruct(shape, BF16),
            jax.ShapeDtypeStruct(shape, F32),
            jax.ShapeDtypeStruct(shape, BF16),
        ],
        in_specs=[
            pl.BlockSpec(memory_space=pltpu.SMEM),
            pl.BlockSpec((S, BLK), lambda b: (0, b)),
            pl.BlockSpec((1, 3 * SLOTS, BLK, BLK), lambda b: (b, 0, 0, 0)),
        ],
        out_specs=[whole, whole, whole],
        scratch_shapes=[pltpu.VMEM((3,) + shape, F32)],
        compiler_params=params(),
        cost_estimate=pl.CostEstimate(flops=4 << 30, bytes_accessed=8 << 20, transcendentals=0),
        name="adjoint",
    )(pattern, probe, sparse)


def forward_kernel(pattern_ref, before_ref, own_ref, after_ref, sparse_ref, out_ref):
    b = pl.program_id(0)
    regions = (before_ref, own_ref, after_ref)
    taken = []
    for s in range(3 * SLOTS):
        start = pl.multiple_of(pattern_ref[b, s] * BLK, BLK)
        taken.append(regions[s // SLOTS][:, pl.ds(start, BLK)])
    left = jnp.concatenate(taken, axis=1)
    right = jnp.concatenate([sparse_ref[0, s] for s in range(3 * SLOTS)], axis=1)
    out_ref[...] = lax.dot_general(
        left, right, (((1,), (1,)), ((), ())), preferred_element_type=F32
    )


def forward(pattern, before, own, after, sparse):
    blocks = sparse.shape[0]
    rows = own.shape[1]
    whole = pl.BlockSpec((S, rows), lambda b: (0, 0))
    return pl.pallas_call(
        forward_kernel,
        grid=(blocks,),
        out_shape=jax.ShapeDtypeStruct((S, rows), F32),
        in_specs=[
            pl.BlockSpec(memory_space=pltpu.SMEM),
            whole,
            whole,
            whole,
            pl.BlockSpec((1, 3 * SLOTS, BLK, BLK), lambda b: (b, 0, 0, 0)),
        ],
        out_specs=pl.BlockSpec((S, BLK), lambda b: (0, b)),
        compiler_params=params(),
        cost_estimate=pl.CostEstimate(flops=4 << 30, bytes_accessed=8 << 20, transcendentals=0),
        name="forward",
    )(pattern, before, own, after, sparse)


def gram_kernel(ext_ref, sparse_ref, own_ref, down_ref, up_ref, samples_ref, gram_ref, sent_ref):
    step = pl.program_id(0)
    width = samples_ref.shape[2]

    @pl.when(step == 0)
    def _():
        gram_ref[...] = jnp.zeros_like(gram_ref)

    for k in range(2):
        y = ext_ref[:, k].reshape(S, width).astype(F32)
        if k == 0:
            y += sparse_ref[...]
        else:
            parts = []
            for c in range(width // BLK):
                parts.append(own_ref[c] + down_ref[c].astype(F32) + up_ref[c].astype(F32))
            y += jnp.concatenate(parts, axis=1)
        samples_ref[k] = y
        gram_ref[k] += lax.dot_general(
            y, y, (((1,), (1,)), ((), ())), precision=HIGHEST, preferred_element_type=F32
        )

    @pl.when(step == pl.num_programs(0) - 1)
    def _():
        sent_ref[...] = gram_ref[...].astype(BF16)


def gram(ext, sparse, own, down, up):
    rows = sparse.shape[1]
    width = 2 * BLK
    leaves, _, here, _ = ext.shape
    terms = pl.BlockSpec((width // BLK, S, BLK), lambda i: (i, 0, 0))
    whole = pl.BlockSpec((2, S, S), lambda i: (0, 0, 0))
    return pl.pallas_call(
        gram_kernel,
        grid=(rows // width,),
        out_shape=[
            jax.ShapeDtypeStruct((2, S, rows), F32),
            jax.ShapeDtypeStruct((2, S, S), F32),
            jax.ShapeDtypeStruct((2, S, S), BF16),
        ],
        in_specs=[
            pl.BlockSpec((leaves, 2, here, width), lambda i: (0, 0, 0, i)),
            pl.BlockSpec((S, width), lambda i: (0, i)),
            terms,
            terms,
            terms,
        ],
        out_specs=[pl.BlockSpec((2, S, width), lambda i: (0, 0, i)), whole, whole],
        compiler_params=params(),
        cost_estimate=pl.CostEstimate(flops=2 << 30, bytes_accessed=7 << 20, transcendentals=0),
        name="gram",
    )(ext, sparse, own, down, up)


def factorize(work, count):
    lane = lax.broadcasted_iota(jnp.int32, (8, BLK), 1)
    for lo in range(0, S, PANEL):
        half = lo // BLK
        rows = [
            [work[b][pl.ds(lo + i, 8, stride=PITCH), :] for b in range(2)] for i in range(PANEL)
        ]
        for j in range(PANEL):
            at = lo + j - half * BLK
            row = rows[j]
            scale = lax.rsqrt(jnp.broadcast_to(row[half][:, at : at + 1], (8, BLK)))
            here = lane == at
            done = [x * scale for x in row]
            done[half] = jnp.where(here, scale, done[half])
            rows[j] = done
            for i in range(j + 1, PANEL):
                to = at + i - j
                factor = jnp.broadcast_to(row[half][:, to : to + 1], (8, BLK)) * scale
                new = []
                for b in range(2):
                    base = rows[i][b]
                    if b == half:
                        base = jnp.where(here, 0.0, base)
                    new.append(base - factor * done[b])
                rows[i] = new
        for i in range(PANEL):
            for b in range(2):
                work[b][pl.ds(lo + i, 8, stride=PITCH), :] = rows[i][b]
        end = lo + PANEL
        if end == S:
            break
        row_id = lax.broadcasted_iota(jnp.int32, (PANEL, BLK), 0) + lo
        col_id = lax.broadcasted_iota(jnp.int32, (PANEL, BLK), 1) + BLK * half
        dead = (col_id > row_id) & (col_id < end)
        cols = lax.broadcasted_iota(jnp.int32, (S - end, BLK), 1) + BLK * half
        mine = (cols >= lo) & (cols < end)
        for m in range(count):
            base = m * PITCH
            panel = [work[b][base + lo : base + end, :] for b in range(2)]
            masked = [jnp.where(dead, 0.0, x) if b == half else x for b, x in enumerate(panel)]
            skip = end // BLK
            left = panel[1] if skip else jnp.concatenate(panel, axis=1)
            lh, lm, ll = split3(left)
            rh, rm, rl = split3(jnp.concatenate(masked, axis=1))
            product = lax.dot_general(
                jnp.concatenate([lh, lh, lm, lh, ll, lm], axis=0),
                jnp.concatenate([rh, rm, rh, rl, rh, rm], axis=0),
                (((0,), (0,)), ((), ())),
                preferred_element_type=F32,
            )[end - skip * BLK :]
            for b in range(2):
                old = work[b][base + end : base + S, :]
                if b == half:
                    old = jnp.where(mine, 0.0, old)
                work[b][base + end : base + S, :] = old - product[:, b * BLK : (b + 1) * BLK]


def factor_kernel(g0_ref, g1_ref, g2_ref, samples_ref, row_ref, col_ref, transfer_ref, w0, w1):
    work = (w0, w1)
    grams = (g0_ref, g1_ref, g2_ref)
    for m in range(8):
        source = grams[m // 2 % 3]
        for b in range(2):
            work[b][m * PITCH : m * PITCH + S, :] = source[m % 2, :, b * BLK : (b + 1) * BLK]
    factorize(work, 6)
    row_id = lax.broadcasted_iota(jnp.int32, (S, S), 0)
    col_id = lax.broadcasted_iota(jnp.int32, (S, S), 1)

    def read(m):
        return jnp.concatenate(
            [work[b][m * PITCH : m * PITCH + S, :] for b in range(2)], axis=1
        )

    gain = math.sqrt(samples_ref.shape[2])
    for k in range(2):
        found = [read(2 * level + k) for level in range(3)]
        inverse = [jnp.where(col_id <= row_id, x, 0.0) for x in found]
        upper = [
            jnp.where(col_id > row_id, x, jnp.where(col_id == row_id, 1.0 / x, 0.0))
            for x in found[:2]
        ]
        basis = dot3(inverse[0], samples_ref[k], ((1,), (0,))) * gain
        (row_ref, col_ref)[k][...] = basis.astype(BF16)
        for level in range(2):
            transfer_ref[k, level] = dot3(upper[level], inverse[level + 1], ((1,), (1,)))


def factor(g0, g1, g2, samples):
    rows = samples.shape[2]
    vmem = pl.BlockSpec(memory_space=pltpu.VMEM)
    return pl.pallas_call(
        factor_kernel,
        out_shape=[
            jax.ShapeDtypeStruct((S, rows), BF16),
            jax.ShapeDtypeStruct((S, rows), BF16),
            jax.ShapeDtypeStruct((2, 2, S, S), F32),
        ],
        in_specs=[vmem] * 4,
        out_specs=[vmem] * 3,
        scratch_shapes=[pltpu.VMEM((8 * PITCH, BLK), F32)] * 2,
        compiler_params=params(),
        name="factor",
    )(g0, g1, g2, samples)


def shifted(block, axis, distance):
    devices = range(lax.axis_size(axis))
    route = [(i - distance, i) for i in devices if i - distance in devices]
    return lax.ppermute(block, axis, route)


def from_partner(value, axis, bit):
    mask = 2**bit
    pairs = [(source, source ^ mask) for source in range(lax.axis_size(axis))]
    return lax.ppermute(value, axis, pairs)


def local(
    child_samples, child_map, forward_probe, adjoint_probe, stored_sparse_blocks, block_pattern
):
    leaves = lax.axis_size("col")
    row_pos = lax.axis_index("row")
    before = shifted(forward_probe, "row", 1)
    after = shifted(forward_probe, "row", -1)
    pattern = lax.dynamic_index_in_dim(block_pattern, row_pos, 0, keepdims=False)
    sent = extend(child_map, child_samples, leaves)
    ext = lax.all_to_all(sent, "col", split_axis=0, concat_axis=0, tiled=True)
    above, own, below = adjoint(pattern, adjoint_probe, stored_sparse_blocks)
    down = shifted(above, "row", -1)
    up = shifted(below, "row", 1)
    sparse = forward(pattern, before, forward_probe, after, stored_sparse_blocks)
    samples, g0, g0_sent = gram(ext, sparse, own, down, up)
    g1 = g0 + from_partner(g0_sent, "col", 0).astype(F32)
    g2 = g1 + from_partner(g1.astype(BF16), "col", 1).astype(F32)
    return tuple(factor(g0, g1, g2, samples))


def solution(mesh):
    return jax.shard_map(
        local,
        mesh=mesh,
        in_specs=(
            P(None, None, "col", "row"),
            P(None, "row"),
            P(None, ("row", "col")),
            P(None, ("row", "col")),
            P(("row", "col"), None, None, None),
            P(None, "col", None),
        ),
        out_specs=(
            P(None, ("row", "col")),
            P(None, ("row", "col")),
            P(None, None, ("row", "col"), None),
        ),
        check_vma=False,
    )
```

time: 535 us -> 96.8 us (0.18)
  the two profiles are of different devices: /device:TPU:96 before, /device:TPU:1 now
where the time goes in v1:
time: 96.8 us; the launch traced here: 96 us
  Pallas kernels  53 us (55%)
  starting transfers between devices  24.4 us (25%)
  waiting for transfers between devices  12.5 us (13%)
  local copies, waits for them, and re-layouts  3.45 us (4%)
  other arithmetic  1.98 us (2%)
    pallas_call x1, Pallas kernels, factor(): pl.pallas_call(factor_kernel, out_shape=[jax.ShapeDtypeStruct((S, rows),...  26.6 us
    ppermute x4, starting transfers between devices, shifted(): return lax.ppermute(block, axis, route)  12.8 us
    ppermute x2, waiting for transfers between devices, from_partner(): return lax.ppermute(value, axis, pairs)  12.4 us
    pallas_call x1, Pallas kernels, adjoint(): pl.pallas_call(adjoint_kernel, grid=(blocks,), out_shape=[jax.ShapeDtypeS...  8.92 us
    pallas_call x1, Pallas kernels, forward(): pl.pallas_call(forward_kernel, grid=(blocks,), out_shape=jax.ShapeDtypeSt...  8.31 us
    all_to_all x1, starting transfers between devices, local(): ext = lax.all_to_all(sent, 'col', split_axis=0, concat_axis=0, tiled=True)  6.75 us
    pallas_call x1, Pallas kernels, gram(): pl.pallas_call(gram_kernel, grid=(rows // width,), out_shape=[jax.ShapeDt...  5.91 us
    ppermute x2, starting transfers between devices, from_partner(): return lax.ppermute(value, axis, pairs)  4.81 us
  transfers between devices with their start and end apart: 7, of which 2 were waited for; matrix products, arithmetic and copies ran while one was open for 1% of the time, Pallas kernels for 21%

profile of v1, /device:TPU:1, one launch (start us, length us, event | category | flops | bytes accessed | tf_op | source)
XLA Modules:
  0.0 96.0 jit_solution(18310593494537680378)
XLA Ops:
  0.6 0.0 copy-start
  0.6 5.1 %collective-permute-start = (bf16[256,1024]{1,0:T(8,128)(2,1)}, bf16[256,1024]{1,0:T(8,128)(2,1)S(1)}, u32[]{:S(2)}, u32[]{:S(2)}) collective-permute-start(bf16[256,1024]{1,0:T(8,128)(2,1)} %own_ref.1), channel_id=1, source_target_pairs={{0,16},{16,32},{32,48},{48,64},{64,80},{80,96},{96,112},{112,128},... | collective-permute-start | bytes 1572872 | tf_op jit(solution)/shard_map/ppermute | solution.py:322
  5.7 1.9 %collective-permute-start.1 = (bf16[256,1024]{1,0:T(8,128)(2,1)}, bf16[256,1024]{1,0:T(8,128)(2,1)S(1)}, u32[]{:S(2)}, u32[]{:S(2)}) collective-permute-start(bf16[256,1024]{1,0:T(8,128)(2,1)} %own_ref.1), channel_id=1, source_target_pairs={{16,0},{32,16},{48,32},{64,48},{80,64},{96,80},{112,96},{128,112},... | collective-permute-start | bytes 1572872 | tf_op jit(solution)/shard_map/ppermute | solution.py:322
  7.6 3.3 %extend.1 = bf16[16,2,16,1024]{3,2,1,0:T(8,128)(2,1)} custom-call(s32[2,128]{1,0:T(2,128)} %map_ref.1, bf16[2,2,16,16384]{3,2,1,0:T(8,128)(2,1)} %child_ref.1), custom_call_target="tpu_custom_call" | custom-call | flops 1048576 | bytes 3145728 | tf_op jit(solution)/shard_map/extend/pallas_call | solution.py:62
  10.9 6.8 %all-to-all-start = ((bf16[16,2,16,1024]{3,2,1,0:T(8,128)(2,1)}), bf16[16,2,16,1024]{3,2,1,0:T(8,128)(2,1)S(1)}, u32[]{:S(2)}, u32[]{:S(2)}) async-start(bf16[16,2,16,1024]{3,2,1,0:T(8,128)(2,1)} %extend.1), calls=%async_computation | async-start | bytes 2097152 | tf_op jit(solution)/shard_map/all_to_all | solution.py:340
  17.7 0.6 dynamic-slice_bitcast_fusion.pattern_ref
  18.3 8.9 %adjoint.1 = (bf16[8,256,128]{2,1,0:T(8,128)(2,1)}, f32[8,256,128]{2,1,0:T(8,128)}, bf16[8,256,128]{2,1,0:T(8,128)(2,1)}) custom-call(s32[8,18]{1,0:T(8,128)} %dynamic-slice_bitcast_fusion.pattern_ref, bf16[256,1024]{1,0:T(8,128)(2,1)} %probe_ref.1, bf16[8,18,128,128]{3,2,1,0:T(8,128)(2,1)} %sparse_ref.3), custom_call_target="tpu_custom_call" | custom-call | flops 4294967296 | bytes 8388608 | tf_op jit(solution)/shard_map/adjoint/pallas_call | solution.py:102
  27.2 1.9 %collective-permute-start.2 = (bf16[8,256,128]{2,1,0:T(8,128)(2,1)}, bf16[8,256,128]{2,1,0:T(8,128)(2,1)S(1)}, u32[]{:S(2)}, u32[]{:S(2)}) collective-permute-start(bf16[8,256,128]{2,1,0:T(8,128)(2,1)} %get-tuple-element.10), channel_id=1, source_target_pairs={{16,0},{32,16},{48,32},{64,48},{80,64},{96,80},{112,96},{128,112},... | collective-permute-start | bytes 1572872 | tf_op jit(solution)/shard_map/ppermute | solution.py:322
  29.1 3.9 %collective-permute-start.3 = (bf16[8,256,128]{2,1,0:T(8,128)(2,1)}, bf16[8,256,128]{2,1,0:T(8,128)(2,1)S(1)}, u32[]{:S(2)}, u32[]{:S(2)}) collective-permute-start(bf16[8,256,128]{2,1,0:T(8,128)(2,1)} %get-tuple-element.11), channel_id=1, source_target_pairs={{0,16},{16,32},{32,48},{48,64},{64,80},{80,96},{96,112},{112,128},... | collective-permute-start | bytes 1572872 | tf_op jit(solution)/shard_map/ppermute | solution.py:322
  33.1 0.8 copy-done.3
  33.9 0.8 copy-done.4
  34.7 8.3 %forward.1.sparse_ref = f32[256,1024]{1,0:T(8,128)} custom-call(s32[8,18]{1,0:T(8,128)} %dynamic-slice_bitcast_fusion.pattern_ref, bf16[256,1024]{1,0:T(8,128)(2,1)} %copy-done.3, bf16[256,1024]{1,0:T(8,128)(2,1)} %own_ref.1, bf16[256,1024]{1,0:T(8,128)(2,1)} %copy-done.4, bf16[8,18,128,128]{3,2,1,0:T(8,128)(2,1)} %sparse_ref.3), custom_call_target="tpu_custom_call" | custom-call | flops 4294967296 | bytes 8388608 | tf_op jit(solution)/shard_map/forward/pallas_call | solution.py:141
  43.0 0.0 copy-start.2
  43.0 0.7 copy-done.5
  43.8 0.2 copy-done.6
  43.9 0.3 copy-done.2
  44.3 5.9 %gram.1 = (f32[2,256,1024]{2,1,0:T(8,128)}, f32[2,256,256]{2,1,0:T(8,128)}, bf16[2,256,256]{2,1,0:T(8,128)(2,1)}) custom-call(bf16[16,2,16,1024]{3,2,1,0:T(8,128)(2,1)} %copy-done.2, f32[256,1024]{1,0:T(8,128)} %forward.1.sparse_ref, f32[8,256,128]{2,1,0:T(8,128)} %get-tuple-element.9.own_ref, bf16[8,256,128]{2,1,0:T(8,128)(2,1)} %copy-done.5, ...), custom_call_target="tpu_custom_call" | custom-call | flops 2147483648 | bytes 7340032 | tf_op jit(solution)/shard_map/gram/pallas_call | solution.py:192
  50.2 1.7 %collective-permute-start.4 = (bf16[2,256,256]{2,1,0:T(8,128)(2,1)}, bf16[2,256,256]{2,1,0:T(8,128)(2,1)S(1)}, u32[]{:S(2)}, u32[]{:S(2)}) collective-permute-start(bf16[2,256,256]{2,1,0:T(8,128)(2,1)} %get-tuple-element.13), channel_id=1, source_target_pairs={{0,1},{1,0},{2,3},{3,2},{4,5},{5,4},{6,7},{7,6},{8,9},{9,8},{10,11... | collective-permute-start | bytes 786440 | tf_op jit(solution)/shard_map/ppermute | solution.py:328
  51.9 5.6 %collective-permute-done.4 = bf16[2,256,256]{2,1,0:T(8,128)(2,1)S(1)} collective-permute-done((bf16[2,256,256]{2,1,0:T(8,128)(2,1)}, bf16[2,256,256]{2,1,0:T(8,128)(2,1)S(1)}, u32[]{:S(2)}, u32[]{:S(2)}) %collective-permute-start.4) | collective-permute-done | bytes 262176 | tf_op jit(solution)/shard_map/ppermute | solution.py:328
  57.5 1.1 %fusion = (bf16[2,256,256]{2,1,0:T(8,128)(2,1)S(1)}, f32[2,256,256]{2,1,0:T(8,128)S(1)}) fusion(f32[2,256,256]{2,1,0:T(8,128)} %get-tuple-element.12.g0_ref, bf16[2,256,256]{2,1,0:T(8,128)(2,1)S(1)} %collective-permute-done.4), kind=kLoop, calls=%fused_computation.3 | loop fusion | flops 393216 | bytes 1572864 | tf_op jit(solution)/shard_map/convert_element_type | solution.py:347
  58.6 3.1 %collective-permute-start.5 = (bf16[2,256,256]{2,1,0:T(8,128)(2,1)S(1)}, bf16[2,256,256]{2,1,0:T(8,128)(2,1)S(1)}, u32[]{:S(2)}, u32[]{:S(2)}) collective-permute-start(bf16[2,256,256]{2,1,0:T(8,128)(2,1)S(1)} %get-tuple-element.15), channel_id=1, source_target_pairs={{0,2},{1,3},{2,0},{3,1},{4,6},{5,7},{6,4},{7,5},{8,10},{9,11},{10,... | collective-permute-start | bytes 786440 | tf_op jit(solution)/shard_map/ppermute | solution.py:328
  61.7 6.9 %collective-permute-done.5 = bf16[2,256,256]{2,1,0:T(8,128)(2,1)S(1)} collective-permute-done((bf16[2,256,256]{2,1,0:T(8,128)(2,1)S(1)}, bf16[2,256,256]{2,1,0:T(8,128)(2,1)S(1)}, u32[]{:S(2)}, u32[]{:S(2)}) %collective-permute-start.5) | collective-permute-done | bytes 262176 | tf_op jit(solution)/shard_map/ppermute | solution.py:328
  68.6 0.9 convert_add_fusion.g2_ref
  69.4 26.6 %factor.1 = (bf16[256,1024]{1,0:T(8,128)(2,1)}, bf16[256,1024]{1,0:T(8,128)(2,1)}, f32[2,2,256,256]{3,2,1,0:T(8,128)}) custom-call(f32[2,256,256]{2,1,0:T(8,128)} %get-tuple-element.12.g0_ref, f32[2,256,256]{2,1,0:T(8,128)} %copy-done.1, f32[2,256,256]{2,1,0:T(8,128)} %convert_add_fusion.g2_ref, f32[2,256,1024]{2,1,0:T(8,128)} %get-tuple-element.14.samples_ref), custom_call_target="tpu_custom_call" | custom-call | tf_op jit(solution)/shard_map/factor/pallas_call | solution.py:304
  (12 shorter events, 0.0 us)
Async XLA Ops:
  0.6 17.1 %copy-start = (s32[16,8,18]{2,1,0:T(8,128)S(1)}, s32[16,8,18]{2,1,0:T(8,128)}, u32[]{:S(2)}) copy-start(s32[16,8,18]{2,1,0:T(8,128)} %param.11) | copy-start | bytes 27652
  0.6 32.4 %collective-permute-start = (bf16[256,1024]{1,0:T(8,128)(2,1)}, bf16[256,1024]{1,0:T(8,128)(2,1)S(1)}, u32[]{:S(2)}, u32[]{:S(2)}) collective-permute-start(bf16[256,1024]{1,0:T(8,128)(2,1)} %own_ref.1), channel_id=1, source_target_pairs={{0,16},{16,32},{32,48},{48,64},{64,80},{80,96},{96,112},{112,128},... | collective-permute-start | bytes 1572872 | tf_op jit(solution)/shard_map/ppermute | solution.py:322
  5.7 27.4 %collective-permute-start.1 = (bf16[256,1024]{1,0:T(8,128)(2,1)}, bf16[256,1024]{1,0:T(8,128)(2,1)S(1)}, u32[]{:S(2)}, u32[]{:S(2)}) collective-permute-start(bf16[256,1024]{1,0:T(8,128)(2,1)} %own_ref.1), channel_id=1, source_target_pairs={{16,0},{32,16},{48,32},{64,48},{80,64},{96,80},{112,96},{128,112},... | collective-permute-start | bytes 1572872 | tf_op jit(solution)/shard_map/ppermute | solution.py:322
  10.9 32.1 %all-to-all-start = ((bf16[16,2,16,1024]{3,2,1,0:T(8,128)(2,1)}), bf16[16,2,16,1024]{3,2,1,0:T(8,128)(2,1)S(1)}, u32[]{:S(2)}, u32[]{:S(2)}) async-start(bf16[16,2,16,1024]{3,2,1,0:T(8,128)(2,1)} %extend.1), calls=%async_computation | async-start | bytes 2097152 | tf_op jit(solution)/shard_map/all_to_all | solution.py:340
  27.2 15.8 %collective-permute-start.2 = (bf16[8,256,128]{2,1,0:T(8,128)(2,1)}, bf16[8,256,128]{2,1,0:T(8,128)(2,1)S(1)}, u32[]{:S(2)}, u32[]{:S(2)}) collective-permute-start(bf16[8,256,128]{2,1,0:T(8,128)(2,1)} %get-tuple-element.10), channel_id=1, source_target_pairs={{16,0},{32,16},{48,32},{64,48},{80,64},{96,80},{112,96},{128,112},... | collective-permute-start | bytes 1572872 | tf_op jit(solution)/shard_map/ppermute | solution.py:322
  29.1 13.9 %collective-permute-start.3 = (bf16[8,256,128]{2,1,0:T(8,128)(2,1)}, bf16[8,256,128]{2,1,0:T(8,128)(2,1)S(1)}, u32[]{:S(2)}, u32[]{:S(2)}) collective-permute-start(bf16[8,256,128]{2,1,0:T(8,128)(2,1)} %get-tuple-element.11), channel_id=1, source_target_pairs={{0,16},{16,32},{32,48},{48,64},{64,80},{80,96},{96,112},{112,128},... | collective-permute-start | bytes 1572872 | tf_op jit(solution)/shard_map/ppermute | solution.py:322
  33.1 0.8 copy-start.3
  33.9 0.8 copy-start.4
  43.0 0.8 copy-start.5
  43.0 1.0 copy-start.6
  43.0 1.3 %copy-start.2 = (bf16[16,2,16,1024]{3,2,1,0:T(8,128)(2,1)}, bf16[16,2,16,1024]{3,2,1,0:T(8,128)(2,1)S(1)}, u32[]{:S(2)}) copy-start(bf16[16,2,16,1024]{3,2,1,0:T(8,128)(2,1)S(1)} %all-to-all-done.ext_ref) | copy-start | bytes 3145732
  50.2 7.3 %collective-permute-start.4 = (bf16[2,256,256]{2,1,0:T(8,128)(2,1)}, bf16[2,256,256]{2,1,0:T(8,128)(2,1)S(1)}, u32[]{:S(2)}, u32[]{:S(2)}) collective-permute-start(bf16[2,256,256]{2,1,0:T(8,128)(2,1)} %get-tuple-element.13), channel_id=1, source_target_pairs={{0,1},{1,0},{2,3},{3,2},{4,5},{5,4},{6,7},{7,6},{8,9},{9,8},{10,11... | collective-permute-start | bytes 786440 | tf_op jit(solution)/shard_map/ppermute | solution.py:328
  58.6 10.9 %copy-start.1 = (f32[2,256,256]{2,1,0:T(8,128)}, f32[2,256,256]{2,1,0:T(8,128)S(1)}, u32[]{:S(2)}) copy-start(f32[2,256,256]{2,1,0:T(8,128)S(1)} %get-tuple-element.16.g1_ref) | copy-start | bytes 1572868
  58.6 10.0 %collective-permute-start.5 = (bf16[2,256,256]{2,1,0:T(8,128)(2,1)S(1)}, bf16[2,256,256]{2,1,0:T(8,128)(2,1)S(1)}, u32[]{:S(2)}, u32[]{:S(2)}) collective-permute-start(bf16[2,256,256]{2,1,0:T(8,128)(2,1)S(1)} %get-tuple-element.15), channel_id=1, source_target_pairs={{0,2},{1,3},{2,0},{3,1},{4,6},{5,7},{6,4},{7,5},{8,10},{9,11},{10,... | collective-permute-start | bytes 786440 | tf_op jit(solution)/shard_map/ppermute | solution.py:328

commit v2 on v1

v2 whole, which is shorter than its diff:
```python
import math

import jax
import jax.numpy as jnp
from jax import lax
from jax.experimental import pallas as pl
from jax.experimental.pallas import tpu as pltpu
from jax.sharding import PartitionSpec as P

S = 256
BLK = 128
SLOTS = 6
PANEL = 32
PITCH = S + 8
F32 = jnp.float32
BF16 = jnp.bfloat16
MESH = pl.DeviceIdType.MESH
VMEM_LIMIT = 56 << 20


def params():
    return pltpu.CompilerParams(vmem_limit_bytes=VMEM_LIMIT)


def split3(x):
    high = x.astype(BF16)
    rest = x - high.astype(F32)
    mid = rest.astype(BF16)
    low = (rest - mid.astype(F32)).astype(BF16)
    return high, mid, low


def dot3(a, b, dims):
    ah, am, _ = split3(a)
    bh, bm, _ = split3(b)
    dn = (dims, ((), ()))
    out = lax.dot_general(ah, bh, dn, preferred_element_type=F32)
    out += lax.dot_general(ah, bm, dn, preferred_element_type=F32)
    out += lax.dot_general(am, bh, dn, preferred_element_type=F32)
    return out


def terms_kernel(
    pattern_ref, map_ref, probe_ref, forward_ref, sparse_ref, child_ref,
    sent_ref, above_ref, own_ref, below_ref, blocked_ref,
    acc0, acc1, acc2, child, child_sem,
):
    b = pl.program_id(0)
    steps = pl.num_programs(0)
    accs = (acc0, acc1, acc2)
    fetch = pltpu.make_async_copy(child_ref, child, child_sem)

    @pl.when(b == 0)
    def _():
        fetch.start()
        for acc in accs:
            acc[...] = jnp.zeros_like(acc)

    blocked_ref[0] = forward_ref[...]
    probe = probe_ref[...]
    for s in range(0, SLOTS, 2):
        for q in range(3):
            slot = q * SLOTS + s
            pair = jnp.concatenate([sparse_ref[0, slot], sparse_ref[0, slot + 1]], axis=1)
            product = jnp.dot(probe, pair, preferred_element_type=F32)
            for i in range(2):
                target = pattern_ref[b, slot + i]
                accs[q][target] += product[:, i * BLK : (i + 1) * BLK]

    leaves = sent_ref.shape[0]
    blocks = sent_ref.shape[3] // BLK
    first_step = 4
    share = leaves // 4

    @pl.when(b == first_step)
    def _():
        fetch.wait()

    @pl.when(b >= first_step)
    def _():
        def leaf(i, carry):
            d = (b - first_step) * share + i
            for c in range(blocks):
                first = pl.multiple_of(map_ref[0, d * blocks + c] * BLK, BLK)
                second = pl.multiple_of(map_ref[1, d * blocks + c] * BLK, BLK)
                for k in range(2):
                    x = child[0, k, :, pl.ds(first, BLK)].astype(F32)
                    y = child[1, k, :, pl.ds(second, BLK)].astype(F32)
                    sent_ref[d, k, :, c * BLK : (c + 1) * BLK] = (x + y).astype(BF16)
            return carry

        lax.fori_loop(0, share, leaf, 0)

    @pl.when(b == steps - 1)
    def _():
        above_ref[...] = acc0[...].astype(BF16)
        own_ref[...] = acc1[...]
        below_ref[...] = acc2[...].astype(BF16)


def local_terms(pattern, child_map, probe, forward_probe, sparse, child_samples, leaves):
    blocks = sparse.shape[0]
    samples_here, rows_group = child_samples.shape[2:]
    shape = (blocks, S, BLK)
    sent = (leaves, 2, samples_here, rows_group // leaves)
    whole = pl.BlockSpec(shape, lambda b: (0, 0, 0))
    smem = pl.BlockSpec(memory_space=pltpu.SMEM)
    return pl.pallas_call(
        terms_kernel,
        grid=(blocks,),
        out_shape=[
            jax.ShapeDtypeStruct(sent, BF16),
            jax.ShapeDtypeStruct(shape, BF16),
            jax.ShapeDtypeStruct(shape, F32),
            jax.ShapeDtypeStruct(shape, BF16),
            jax.ShapeDtypeStruct(shape, BF16),
        ],
        in_specs=[
            smem,
            smem,
            pl.BlockSpec((S, BLK), lambda b: (0, b)),
            pl.BlockSpec((S, BLK), lambda b: (0, b)),
            pl.BlockSpec((1, 3 * SLOTS, BLK, BLK), lambda b: (b, 0, 0, 0)),
            pl.BlockSpec(memory_space=pl.ANY),
        ],
        out_specs=[pl.BlockSpec(sent, lambda b: (0, 0, 0, 0)), whole, whole, whole]
        + [pl.BlockSpec((1, S, BLK), lambda b: (b, 0, 0))],
        scratch_shapes=[pltpu.VMEM(shape, F32)] * 3
        + [pltpu.VMEM(child_samples.shape, BF16), pltpu.SemaphoreType.DMA],
        compiler_params=params(),
        name="terms",
    )(pattern, child_map, probe, forward_probe, sparse, child_samples)


def exchange_kernel(
    pattern_ref, probe_ref, sent_ref, above_ref, own_ref, below_ref, sparse_ref,
    samples_ref, gram_ref,
    ext, before, after, down, up, own, blocks, samples, gram, packed, partner,
    ext_send, ext_recv, row_send, row_recv, quad_send, quad_recv, local_sem, block_sem,
):
    row = lax.axis_index("row")
    col = lax.axis_index("col")
    n_row = lax.axis_size("row")
    n_col = lax.axis_size("col")
    n_blocks = blocks.shape[0]
    side = 4
    cx = col // side
    cy = col % side
    inner_up = row < n_row - 1
    inner_down = row > 0

    peers = []
    for d in range(1, n_col):
        px = (cx + d // side) % side
        py = (cy + d % side) % side
        peers.append(px * side + py)

    barrier = pltpu.get_barrier_semaphore()
    for peer in peers:
        pl.semaphore_signal(barrier, inc=1, device_id=(row, peer), device_id_type=MESH)

    for neighbour in ((row + 1) % n_row, (row + n_row - 1) % n_row):
        pl.semaphore_signal(barrier, inc=1, device_id=(neighbour, col), device_id_type=MESH)

    fetches = [
        pltpu.make_async_copy(sparse_ref.at[b], blocks.at[b], block_sem.at[b])
        for b in range(n_blocks)
    ]
    own_fetch = pltpu.make_async_copy(own_ref, own, local_sem.at[0])
    ext_fetch = pltpu.make_async_copy(sent_ref.at[col], ext.at[col], local_sem.at[1])
    for fetch in fetches:
        fetch.start()
    own_fetch.start()
    ext_fetch.start()

    @pl.when(row == 0)
    def _():
        before[...] = jnp.zeros_like(before)
        up[...] = jnp.zeros_like(up)

    @pl.when(row == n_row - 1)
    def _():
        after[...] = jnp.zeros_like(after)
        down[...] = jnp.zeros_like(down)

    def to_row(source, target, index, step):
        return pltpu.make_async_remote_copy(
            src_ref=source,
            dst_ref=target,
            send_sem=row_send.at[index],
            recv_sem=row_recv.at[index],
            device_id=(row + step, col),
            device_id_type=MESH,
        )

    rising = [to_row(probe_ref, before, 0, 1), to_row(below_ref, up, 1, 1)]
    falling = [to_row(probe_ref, after, 2, -1), to_row(above_ref, down, 3, -1)]

    pl.semaphore_wait(barrier, n_col + 1)

    @pl.when(inner_up)
    def _():
        rising[0].start()

    @pl.when(inner_down)
    def _():
        falling[0].start()

    spread = [
        pltpu.make_async_remote_copy(
            src_ref=sent_ref.at[peer],
            dst_ref=ext.at[col],
            send_sem=ext_send.at[i],
            recv_sem=ext_recv.at[i],
            device_id=(row, peer),
            device_id_type=MESH,
        )
        for i, peer in enumerate(peers)
    ]
    for copy in spread:
        copy.start()

    @pl.when(inner_up)
    def _():
        rising[1].start()

    @pl.when(inner_down)
    def _():
        falling[1].start()

    def product(b, regions):
        left = []
        right = []
        for q, source in regions:
            for s in range(q * SLOTS, (q + 1) * SLOTS):
                left.append(source[pattern_ref[b, s]])
                right.append(blocks[b, s])
        return lax.dot_general(
            jnp.concatenate(left, axis=1),
            jnp.concatenate(right, axis=1),
            (((1,), (1,)), ((), ())),
            preferred_element_type=F32,
        )

    for fetch in fetches:
        fetch.wait()

    def own_region(b, carry):
        lanes = pl.ds(pl.multiple_of(b * BLK, BLK), BLK)
        samples[0, :, lanes] = product(b, [(1, probe_ref)])
        return carry

    lax.fori_loop(0, n_blocks, own_region, 0)

    @pl.when(inner_down)
    def _():
        rising[0].wait_recv()

    @pl.when(inner_up)
    def _():
        falling[0].wait_recv()

    def other_regions(b, carry):
        lanes = pl.ds(pl.multiple_of(b * BLK, BLK), BLK)
        samples[0, :, lanes] += product(b, [(0, before), (2, after)])
        return carry

    lax.fori_loop(0, n_blocks, other_regions, 0)

    gram[...] = jnp.zeros_like(gram)
    own_fetch.wait()
    ext_fetch.wait()
    for copy in spread:
        copy.wait_recv()

    @pl.when(inner_down)
    def _():
        rising[1].wait_recv()

    @pl.when(inner_up)
    def _():
        falling[1].wait_recv()

    def assemble(h, carry):
        lanes = pl.ds(pl.multiple_of(h * 2 * BLK, 2 * BLK), 2 * BLK)
        for k in range(2):
            y = ext[:, k, :, lanes].reshape(S, 2 * BLK).astype(F32)
            if k == 0:
                y += samples[0, :, lanes]
            else:
                parts = []
                for c in range(2):
                    at = h * 2 + c
                    parts.append(own[at] + down[at].astype(F32) + up[at].astype(F32))
                y += jnp.concatenate(parts, axis=1)
            samples[k, :, lanes] = y
            gram[k] += dot3(y, y, ((1,), (1,)))
        return carry

    lax.fori_loop(0, n_blocks // 2, assemble, 0)

    row_id = lax.broadcasted_iota(jnp.int32, (BLK, BLK), 0)
    col_id = lax.broadcasted_iota(jnp.int32, (BLK, BLK), 1)
    for k in range(2):
        last = gram[k, BLK:, BLK:]
        diagonal = jnp.sum(jnp.where(row_id == col_id, last, 0.0), axis=0, keepdims=True)
        pieces = (
            (0, gram[k, :BLK, BLK:]),
            (BLK, jnp.where(col_id >= row_id, gram[k, :BLK, :BLK], last)),
            (2 * BLK, jnp.broadcast_to(diagonal, (16, BLK))),
        )
        for at, piece in pieces:
            gram_ref[0, k, at : at + piece.shape[0]] = piece
            packed[k, at : at + piece.shape[0]] = piece.astype(BF16)

    quad = [
        pltpu.make_async_remote_copy(
            src_ref=packed,
            dst_ref=partner.at[i],
            send_sem=quad_send.at[i],
            recv_sem=quad_recv.at[i],
            device_id=(row, cx * side + other),
            device_id_type=MESH,
        )
        for i, other in enumerate(
            (cy + 1 - 2 * (cy % 2), (cy + 2) % side, side - 1 - cy)
        )
    ]
    for copy in quad:
        copy.start()
    store = pltpu.make_async_copy(samples, samples_ref, local_sem.at[2])
    store.start()

    @pl.when(inner_up)
    def _():
        for copy in rising:
            copy.wait_send()

    @pl.when(inner_down)
    def _():
        for copy in falling:
            copy.wait_send()

    for copy in spread:
        copy.wait_send()
    quad[0].wait_recv()
    for k in range(2):
        gram_ref[1, k] = gram_ref[0, k] + partner[0, k].astype(F32)
    quad[1].wait_recv()
    quad[2].wait_recv()
    for k in range(2):
        gram_ref[2, k] = gram_ref[1, k] + partner[1, k].astype(F32) + partner[2, k].astype(F32)
    for copy in quad:
        copy.wait_send()
    store.wait()


def exchange(pattern, probe, sent, above, own, below, sparse):
    rows = sent.shape[3]
    leaves = sent.shape[0]
    held = 2 * BLK + 16
    anywhere = pl.BlockSpec(memory_space=pl.ANY)
    vmem = pl.BlockSpec(memory_space=pltpu.VMEM)
    dma = pltpu.SemaphoreType.DMA
    return pl.pallas_call(
        exchange_kernel,
        out_shape=[
            jax.ShapeDtypeStruct((2, S, rows), F32),
            jax.ShapeDtypeStruct((3, 2, held, BLK), F32),
        ],
        in_specs=[pl.BlockSpec(memory_space=pltpu.SMEM), vmem] + [anywhere] * 5,
        out_specs=[anywhere, vmem],
        scratch_shapes=[
            pltpu.VMEM(sent.shape, BF16),
            pltpu.VMEM(probe.shape, BF16),
            pltpu.VMEM(probe.shape, BF16),
            pltpu.VMEM(above.shape, BF16),
            pltpu.VMEM(below.shape, BF16),
            pltpu.VMEM(own.shape, F32),
            pltpu.VMEM(sparse.shape, BF16),
            pltpu.VMEM((2, S, rows), F32),
            pltpu.VMEM((2, S, S), F32),
            pltpu.VMEM((2, held, BLK), BF16),
            pltpu.VMEM((3, 2, held, BLK), BF16),
            dma((leaves - 1,)),
            dma((leaves - 1,)),
            dma((4,)),
            dma((4,)),
            dma((3,)),
            dma((3,)),
            dma((3,)),
            dma((sparse.shape[0],)),
        ],
        compiler_params=pltpu.CompilerParams(
            collective_id=0, has_side_effects=True, vmem_limit_bytes=VMEM_LIMIT
        ),
        name="exchange",
    )(pattern, probe, sent, above, own, below, sparse)


def factorize(work, count):
    lane = lax.broadcasted_iota(jnp.int32, (8, BLK), 1)
    for lo in range(0, S, PANEL):
        half = lo // BLK
        rows = [
            [work[b][pl.ds(lo + i, 8, stride=PITCH), :] for b in range(2)] for i in range(PANEL)
        ]
        for j in range(PANEL):
            at = lo + j - half * BLK
            row = rows[j]
            scale = lax.rsqrt(jnp.broadcast_to(row[half][:, at : at + 1], (8, BLK)))
            here = lane == at
            done = [x * scale for x in row]
            done[half] = jnp.where(here, scale, done[half])
            rows[j] = done
            for i in range(j + 1, PANEL):
                to = at + i - j
                factor = jnp.broadcast_to(row[half][:, to : to + 1], (8, BLK)) * scale
                new = []
                for b in range(2):
                    base = rows[i][b]
                    if b == half:
                        base = jnp.where(here, 0.0, base)
                    new.append(base - factor * done[b])
                rows[i] = new
        for i in range(PANEL):
            for b in range(2):
                work[b][pl.ds(lo + i, 8, stride=PITCH), :] = rows[i][b]
        end = lo + PANEL
        if end == S:
            break
        row_id = lax.broadcasted_iota(jnp.int32, (PANEL, BLK), 0) + lo
        col_id = lax.broadcasted_iota(jnp.int32, (PANEL, BLK), 1) + BLK * half
        dead = (col_id > row_id) & (col_id < end)
        cols = lax.broadcasted_iota(jnp.int32, (S - end, BLK), 1) + BLK * half
        mine = (cols >= lo) & (cols < end)
        for m in range(count):
            base = m * PITCH
            panel = [work[b][base + lo : base + end, :] for b in range(2)]
            masked = [jnp.where(dead, 0.0, x) if b == half else x for b, x in enumerate(panel)]
            skip = end // BLK
            left = panel[1] if skip else jnp.concatenate(panel, axis=1)
            lh, lm, ll = split3(left)
            rh, rm, rl = split3(jnp.concatenate(masked, axis=1))
            product = lax.dot_general(
                jnp.concatenate([lh, lh, lm, lh, ll, lm], axis=0),
                jnp.concatenate([rh, rm, rh, rl, rh, rm], axis=0),
                (((0,), (0,)), ((), ())),
                preferred_element_type=F32,
            )[end - skip * BLK :]
            for b in range(2):
                old = work[b][base + end : base + S, :]
                if b == half:
                    old = jnp.where(mine, 0.0, old)
                work[b][base + end : base + S, :] = old - product[:, b * BLK : (b + 1) * BLK]


def factor_kernel(gram_ref, samples_ref, row_ref, col_ref, transfer_ref, w0, w1):
    work = (w0, w1)
    corner_row = lax.broadcasted_iota(jnp.int32, (BLK, BLK), 0)
    corner_col = lax.broadcasted_iota(jnp.int32, (BLK, BLK), 1)
    for m in range(8):
        held = gram_ref.at[m // 2 % 3, m % 2]
        shared = held[BLK : 2 * BLK]
        at = m * PITCH
        w0[at : at + BLK, :] = shared
        w1[at : at + BLK, :] = held[:BLK]
        w1[at + BLK : at + S, :] = jnp.where(
            corner_row == corner_col,
            jnp.broadcast_to(held[2 * BLK : 2 * BLK + 1], (BLK, BLK)),
            shared.T,
        )
        w0[at + BLK : at + S, :] = jnp.zeros((BLK, BLK), F32)
    factorize(work, 6)
    row_id = lax.broadcasted_iota(jnp.int32, (S, S), 0)
    col_id = lax.broadcasted_iota(jnp.int32, (S, S), 1)

    def read(m):
        return jnp.concatenate(
            [work[b][m * PITCH : m * PITCH + S, :] for b in range(2)], axis=1
        )

    gain = math.sqrt(samples_ref.shape[2])
    for k in range(2):
        found = [read(2 * level + k) for level in range(3)]
        inverse = [jnp.where(col_id <= row_id, x, 0.0) for x in found]
        upper = [
            jnp.where(col_id > row_id, x, jnp.where(col_id == row_id, 1.0 / x, 0.0))
            for x in found[:2]
        ]
        basis = dot3(inverse[0], samples_ref[k], ((1,), (0,))) * gain
        (row_ref, col_ref)[k][...] = basis.astype(BF16)
        for level in range(2):
            transfer_ref[k, level] = dot3(upper[level], inverse[level + 1], ((1,), (1,)))


def factor(grams, samples):
    rows = samples.shape[2]
    vmem = pl.BlockSpec(memory_space=pltpu.VMEM)
    return pl.pallas_call(
        factor_kernel,
        out_shape=[
            jax.ShapeDtypeStruct((S, rows), BF16),
            jax.ShapeDtypeStruct((S, rows), BF16),
            jax.ShapeDtypeStruct((2, 2, S, S), F32),
        ],
        in_specs=[vmem] * 2,
        out_specs=[vmem] * 3,
        scratch_shapes=[pltpu.VMEM((8 * PITCH, BLK), F32)] * 2,
        compiler_params=params(),
        name="factor",
    )(grams, samples)


def local(
    child_samples, child_map, forward_probe, adjoint_probe, stored_sparse_blocks, block_pattern
):
    leaves = lax.axis_size("col")
    row_pos = lax.axis_index("row")
    pattern = lax.dynamic_index_in_dim(block_pattern, row_pos, 0, keepdims=False)
    sent, above, own, below, blocked = local_terms(
        pattern, child_map, adjoint_probe, forward_probe, stored_sparse_blocks, child_samples, leaves
    )
    samples, grams = exchange(
        pattern, blocked, sent, above, own, below, stored_sparse_blocks
    )
    return tuple(factor(grams, samples))


def solution(mesh):
    return jax.shard_map(
        local,
        mesh=mesh,
        in_specs=(
            P(None, None, "col", "row"),
            P(None, "row"),
            P(None, ("row", "col")),
            P(None, ("row", "col")),
            P(("row", "col"), None, None, None),
            P(None, "col", None),
        ),
        out_specs=(
            P(None, ("row", "col")),
            P(None, ("row", "col")),
            P(None, None, ("row", "col"), None),
        ),
        check_vma=False,
    )
```

time: 96.8 us -> 74 us (0.76)
  the two profiles are of different devices: /device:TPU:1 before, /device:TPU:96 now
where the time goes in v2:
time: 74 us; the launch traced here: 73.7 us
  Pallas kernels  71.6 us (97%)
  local copies, waits for them, and re-layouts  1.42 us (2%)
    pallas_call x1, Pallas kernels, exchange(): pl.pallas_call(exchange_kernel, out_shape=[jax.ShapeDtypeStruct((2, S, ro...  35.2 us
    pallas_call x1, Pallas kernels, factor(): pl.pallas_call(factor_kernel, out_shape=[jax.ShapeDtypeStruct((S, rows),...  26.4 us
    pallas_call x1, Pallas kernels, local_terms(): pl.pallas_call(terms_kernel, grid=(blocks,), out_shape=[jax.ShapeDtypeStr...  10 us

profile of v2, /device:TPU:96, one launch (start us, length us, event | category | flops | bytes accessed | tf_op | source)
XLA Modules:
  0.0 73.7 jit_solution(807755980561129985)
XLA Ops:
  0.6 0.0 copy-start
  0.6 0.8 %copy-done = s32[16,8,18]{2,1,0:T(8,128)S(1)} copy-done((s32[16,8,18]{2,1,0:T(8,128)S(1)}, s32[16,8,18]{2,1,0:T(8,128)}, u32[]{:S(2)}) %copy-start) | copy-done | bytes 9240
  1.5 0.6 dynamic-slice_bitcast_fusion.pattern_ref
  2.1 10.0 %terms.1 = (bf16[16,2,16,1024]{3,2,1,0:T(8,128)(2,1)}, bf16[8,256,128]{2,1,0:T(8,128)(2,1)}, f32[8,256,128]{2,1,0:T(8,128)}, bf16[8,256,128]{2,1,0:T(8,128)(2,1)}, bf16[8,256,128]{2,1,0:T(8,128)(2,1)}) custom-call(s32[8,18]{1,0:T(8,128)} %dynamic-slice_bitcast_fusion.pattern_ref, s32[2,128]{1,0:T(2,128)} %map_ref.1, bf16[256,1024]{1,0:T(8,128)(2,1)} %probe_ref.1, ...), custom_call_target="tpu_custom_call" | custom-call | tf_op jit(solution)/shard_map/terms/pallas_call | solution.py:108
  12.1 35.2 %exchange.1 = (f32[2,256,1024]{2,1,0:T(8,128)}, f32[3,2,272,128]{3,2,1,0:T(8,128)}) custom-call(s32[8,18]{1,0:T(8,128)} %dynamic-slice_bitcast_fusion.pattern_ref, bf16[8,256,128]{2,1,0:T(8,128)(2,1)} %get-tuple-element.10.probe_ref, bf16[16,2,16,1024]{3,2,1,0:T(8,128)(2,1)} %get-tuple-element.11.sent_ref, bf16[8,256,128]{2,1,0:T(8,128)(2,1)} %get-tuple-element.12.above_ref, ...), custom_call_target="tpu_custom_call" | custom-call | tf_op jit(solution)/shard_map/exchange/pallas_call | solution.py:365
  47.3 26.4 %factor.1 = (bf16[256,1024]{1,0:T(8,128)(2,1)}, bf16[256,1024]{1,0:T(8,128)(2,1)}, f32[2,2,256,256]{3,2,1,0:T(8,128)}) custom-call(f32[3,2,272,128]{3,2,1,0:T(8,128)} %get-tuple-element.15.gram_ref, f32[2,256,1024]{2,1,0:T(8,128)} %get-tuple-element.16.samples_ref), custom_call_target="tpu_custom_call" | custom-call | tf_op jit(solution)/shard_map/factor/pallas_call | solution.py:500
Async XLA Ops:
  0.6 0.8 %copy-start = (s32[16,8,18]{2,1,0:T(8,128)S(1)}, s32[16,8,18]{2,1,0:T(8,128)}, u32[]{:S(2)}) copy-start(s32[16,8,18]{2,1,0:T(8,128)} %param.11) | copy-start | bytes 27652

commit v3 on v2

--- a/solution.py
+++ b/solution.py
@@ -10,7 +10,8 @@
 S = 256
 BLK = 128
 SLOTS = 6
-PANEL = 32
+PANEL = 16
+SUB = 8
 PITCH = S + 8
 F32 = jnp.float32
 BF16 = jnp.bfloat16
@@ -398,6 +399,41 @@
     )(pattern, probe, sent, above, own, below, sparse)
 
 
+def splat(x, at):
+    return jnp.broadcast_to(x[:, at:at+1], (8, BLK))
+
+def eliminate(rows, first, half, lane):
+    count=len(rows)
+    for g in range(0, count, SUB):
+        base=first+g
+        e=[[splat(rows[g+j][half], base+i) if i>=j else None for i in range(SUB)] for j in range(SUB)]
+        scale=[]; fac=[]
+        for j in range(SUB):
+            s=lax.rsqrt(e[j][j]); scale.append(s)
+            f=[e[j][i]*s if i>j else None for i in range(SUB)]
+            fac.append(f)
+            for i in range(j+1,SUB):
+                for l in range(i,SUB):
+                    e[i][l]=e[i][l]-f[i]*f[l]
+        clean=[]
+        for j in range(SUB):
+            here=lane==base+j
+            z=[x*scale[j] for x in rows[g+j]]
+            z[half]=jnp.where(here,scale[j],z[half])
+            rows[g+j]=z
+            for i in range(j+1,SUB):
+                r=list(rows[g+i]); r[half]=jnp.where(here,0.0,r[half])
+                rows[g+i]=[x-fac[j][i]*y for x,y in zip(r,z)]
+            c=list(z); c[half]=jnp.where((lane>base+j)&(lane<base+SUB),0.0,z[half]); clean.append(c)
+        for i in range(g+SUB,count):
+            r=list(rows[i]); r[half]=jnp.where((lane>=base)&(lane<base+SUB),0.0,r[half])
+            for j in range(SUB):
+                z=clean[j]
+                f=splat(z[half], first+i)
+                r=[x-f*y for x,y in zip(r,z)]
+            rows[i]=r
+    return rows
+
 def factorize(work, count):
     lane = lax.broadcasted_iota(jnp.int32, (8, BLK), 1)
     for lo in range(0, S, PANEL):
@@ -405,24 +441,7 @@
         rows = [
             [work[b][pl.ds(lo + i, 8, stride=PITCH), :] for b in range(2)] for i in range(PANEL)
         ]
-        for j in range(PANEL):
-            at = lo + j - half * BLK
-            row = rows[j]
-            scale = lax.rsqrt(jnp.broadcast_to(row[half][:, at : at + 1], (8, BLK)))
-            here = lane == at
-            done = [x * scale for x in row]
-            done[half] = jnp.where(here, scale, done[half])
-            rows[j] = done
-            for i in range(j + 1, PANEL):
-                to = at + i - j
-                factor = jnp.broadcast_to(row[half][:, to : to + 1], (8, BLK)) * scale
-                new = []
-                for b in range(2):
-                    base = rows[i][b]
-                    if b == half:
-                        base = jnp.where(here, 0.0, base)
-                    new.append(base - factor * done[b])
-                rows[i] = new
+        rows = eliminate(rows, lo - half*BLK, half, lane)
         for i in range(PANEL):
             for b in range(2):
                 work[b][pl.ds(lo + i, 8, stride=PITCH), :] = rows[i][b]

time: 74 us -> 62.8 us (0.85)
  Pallas kernels: 71.6 us -> 60.4 us
    pallas_call x1, Pallas kernels: 26.4 us -> 15.4 us  [factor(): pl.pallas_call(factor_kernel, out_shape=[jax.ShapeDtypeStruct((S, rows),...]
where the time goes in v3:
time: 62.8 us; the launch traced here: 62.5 us
  Pallas kernels  60.4 us (96%)
  local copies, waits for them, and re-layouts  1.42 us (2%)
  between operations  0.66 us (1%)
    pallas_call x1, Pallas kernels, exchange(): pl.pallas_call(exchange_kernel, out_shape=[jax.ShapeDtypeStruct((2, S, ro...  34.9 us
    pallas_call x1, Pallas kernels, factor(): pl.pallas_call(factor_kernel, out_shape=[jax.ShapeDtypeStruct((S, rows),...  15.4 us
    pallas_call x1, Pallas kernels, local_terms(): pl.pallas_call(terms_kernel, grid=(blocks,), out_shape=[jax.ShapeDtypeStr...  10 us

profile of v3, /device:TPU:96, one launch (start us, length us, event | category | flops | bytes accessed | tf_op | source)
XLA Modules:
  0.0 62.5 jit_solution(13460469060533065170)
XLA Ops:
  0.6 0.0 copy-start
  0.6 0.8 %copy-done = s32[16,8,18]{2,1,0:T(8,128)S(1)} copy-done((s32[16,8,18]{2,1,0:T(8,128)S(1)}, s32[16,8,18]{2,1,0:T(8,128)}, u32[]{:S(2)}) %copy-start) | copy-done | bytes 9240
  1.5 0.6 dynamic-slice_bitcast_fusion.pattern_ref
  2.1 10.0 %terms.1 = (bf16[16,2,16,1024]{3,2,1,0:T(8,128)(2,1)}, bf16[8,256,128]{2,1,0:T(8,128)(2,1)}, f32[8,256,128]{2,1,0:T(8,128)}, bf16[8,256,128]{2,1,0:T(8,128)(2,1)}, bf16[8,256,128]{2,1,0:T(8,128)(2,1)}) custom-call(s32[8,18]{1,0:T(8,128)} %dynamic-slice_bitcast_fusion.pattern_ref, s32[2,128]{1,0:T(2,128)} %map_ref.1, bf16[256,1024]{1,0:T(8,128)(2,1)} %probe_ref.1, ...), custom_call_target="tpu_custom_call" | custom-call | tf_op jit(solution)/shard_map/terms/pallas_call | solution.py:109
  12.1 34.9 %exchange.1 = (f32[2,256,1024]{2,1,0:T(8,128)}, f32[3,2,272,128]{3,2,1,0:T(8,128)}) custom-call(s32[8,18]{1,0:T(8,128)} %dynamic-slice_bitcast_fusion.pattern_ref, bf16[8,256,128]{2,1,0:T(8,128)(2,1)} %get-tuple-element.10.probe_ref, bf16[16,2,16,1024]{3,2,1,0:T(8,128)(2,1)} %get-tuple-element.11.sent_ref, bf16[8,256,128]{2,1,0:T(8,128)(2,1)} %get-tuple-element.12.above_ref, ...), custom_call_target="tpu_custom_call" | custom-call | tf_op jit(solution)/shard_map/exchange/pallas_call | solution.py:366
  47.1 15.4 %factor.1 = (bf16[256,1024]{1,0:T(8,128)(2,1)}, bf16[256,1024]{1,0:T(8,128)(2,1)}, f32[2,2,256,256]{3,2,1,0:T(8,128)}) custom-call(f32[3,2,272,128]{3,2,1,0:T(8,128)} %get-tuple-element.15.gram_ref, f32[2,256,1024]{2,1,0:T(8,128)} %get-tuple-element.16.samples_ref), custom_call_target="tpu_custom_call" | custom-call | tf_op jit(solution)/shard_map/factor/pallas_call | solution.py:519
Async XLA Ops:
  0.6 0.8 %copy-start = (s32[16,8,18]{2,1,0:T(8,128)S(1)}, s32[16,8,18]{2,1,0:T(8,128)}, u32[]{:S(2)}) copy-start(s32[16,8,18]{2,1,0:T(8,128)} %param.11) | copy-start | bytes 27652

commit v4 on v3

--- a/solution.py
+++ b/solution.py
@@ -48,6 +48,7 @@
 ):
     b = pl.program_id(0)
     steps = pl.num_programs(0)
+    row = lax.axis_index("row")
     accs = (acc0, acc1, acc2)
     fetch = pltpu.make_async_copy(child_ref, child, child_sem)
 
@@ -65,7 +66,7 @@
             pair = jnp.concatenate([sparse_ref[0, slot], sparse_ref[0, slot + 1]], axis=1)
             product = jnp.dot(probe, pair, preferred_element_type=F32)
             for i in range(2):
-                target = pattern_ref[b, slot + i]
+                target = pattern_ref[row, b, slot + i]
                 accs[q][target] += product[:, i * BLK : (i + 1) * BLK]
 
     leaves = sent_ref.shape[0]
@@ -221,20 +222,12 @@
     for copy in spread:
         copy.start()
 
-    @pl.when(inner_up)
-    def _():
-        rising[1].start()
-
-    @pl.when(inner_down)
-    def _():
-        falling[1].start()
-
     def product(b, regions):
         left = []
         right = []
         for q, source in regions:
             for s in range(q * SLOTS, (q + 1) * SLOTS):
-                left.append(source[pattern_ref[b, s]])
+                left.append(source[pattern_ref[row, b, s]])
                 right.append(blocks[b, s])
         return lax.dot_general(
             jnp.concatenate(left, axis=1),
@@ -261,6 +254,14 @@
     def _():
         falling[0].wait_recv()
 
+    @pl.when(inner_up)
+    def _():
+        rising[1].start()
+
+    @pl.when(inner_down)
+    def _():
+        falling[1].start()
+
     def other_regions(b, carry):
         lanes = pl.ds(pl.multiple_of(b * BLK, BLK), BLK)
         samples[0, :, lanes] += product(b, [(0, before), (2, after)])
@@ -269,40 +270,19 @@
     lax.fori_loop(0, n_blocks, other_regions, 0)
 
     gram[...] = jnp.zeros_like(gram)
-    own_fetch.wait()
-    ext_fetch.wait()
-    for copy in spread:
-        copy.wait_recv()
-
-    @pl.when(inner_down)
-    def _():
-        rising[1].wait_recv()
-
-    @pl.when(inner_up)
-    def _():
-        falling[1].wait_recv()
-
-    def assemble(h, carry):
-        lanes = pl.ds(pl.multiple_of(h * 2 * BLK, 2 * BLK), 2 * BLK)
-        for k in range(2):
-            y = ext[:, k, :, lanes].reshape(S, 2 * BLK).astype(F32)
-            if k == 0:
-                y += samples[0, :, lanes]
-            else:
-                parts = []
-                for c in range(2):
-                    at = h * 2 + c
-                    parts.append(own[at] + down[at].astype(F32) + up[at].astype(F32))
-                y += jnp.concatenate(parts, axis=1)
+    row_id = lax.broadcasted_iota(jnp.int32, (BLK, BLK), 0)
+    col_id = lax.broadcasted_iota(jnp.int32, (BLK, BLK), 1)
+    quad = []
+
+    def finish(k, other_terms):
+        def assemble(h, carry):
+            lanes = pl.ds(pl.multiple_of(h * 2 * BLK, 2 * BLK), 2 * BLK)
+            y = ext[:, k, :, lanes].reshape(S, 2 * BLK).astype(F32) + other_terms(h, lanes)
             samples[k, :, lanes] = y
             gram[k] += dot3(y, y, ((1,), (1,)))
-        return carry
-
-    lax.fori_loop(0, n_blocks // 2, assemble, 0)
-
-    row_id = lax.broadcasted_iota(jnp.int32, (BLK, BLK), 0)
-    col_id = lax.broadcasted_iota(jnp.int32, (BLK, BLK), 1)
-    for k in range(2):
+            return carry
+
+        lax.fori_loop(0, n_blocks // 2, assemble, 0)
         last = gram[k, BLK:, BLK:]
         diagonal = jnp.sum(jnp.where(row_id == col_id, last, 0.0), axis=0, keepdims=True)
         pieces = (
@@ -313,22 +293,43 @@
         for at, piece in pieces:
             gram_ref[0, k, at : at + piece.shape[0]] = piece
             packed[k, at : at + piece.shape[0]] = piece.astype(BF16)
-
-    quad = [
-        pltpu.make_async_remote_copy(
-            src_ref=packed,
-            dst_ref=partner.at[i],
-            send_sem=quad_send.at[i],
-            recv_sem=quad_recv.at[i],
-            device_id=(row, cx * side + other),
-            device_id_type=MESH,
-        )
-        for i, other in enumerate(
-            (cy + 1 - 2 * (cy % 2), (cy + 2) % side, side - 1 - cy)
-        )
-    ]
-    for copy in quad:
-        copy.start()
+        copies = [
+            pltpu.make_async_remote_copy(
+                src_ref=packed.at[k],
+                dst_ref=partner.at[i, k],
+                send_sem=quad_send.at[3 * k + i],
+                recv_sem=quad_recv.at[3 * k + i],
+                device_id=(row, cx * side + other),
+                device_id_type=MESH,
+            )
+            for i, other in enumerate((cy + 1 - 2 * (cy % 2), (cy + 2) % side, side - 1 - cy))
+        ]
+        for copy in copies:
+            copy.start()
+        quad.append(copies)
+
+    ext_fetch.wait()
+    for copy in spread:
+        copy.wait_recv()
+    finish(0, lambda h, lanes: samples[0, :, lanes])
+    own_fetch.wait()
+
+    @pl.when(inner_down)
+    def _():
+        rising[1].wait_recv()
+
+    @pl.when(inner_up)
+    def _():
+        falling[1].wait_recv()
+
+    def adjoint_terms(h, lanes):
+        parts = []
+        for c in range(2):
+            at = h * 2 + c
+            parts.append(own[at] + down[at].astype(F32) + up[at].astype(F32))
+        return jnp.concatenate(parts, axis=1)
+
+    finish(1, adjoint_terms)
     store = pltpu.make_async_copy(samples, samples_ref, local_sem.at[2])
     store.start()
 
@@ -344,15 +345,15 @@
 
     for copy in spread:
         copy.wait_send()
-    quad[0].wait_recv()
     for k in range(2):
+        quad[k][0].wait_recv()
         gram_ref[1, k] = gram_ref[0, k] + partner[0, k].astype(F32)
-    quad[1].wait_recv()
-    quad[2].wait_recv()
-    for k in range(2):
+        quad[k][1].wait_recv()
+        quad[k][2].wait_recv()
         gram_ref[2, k] = gram_ref[1, k] + partner[1, k].astype(F32) + partner[2, k].astype(F32)
-    for copy in quad:
-        copy.wait_send()
+    for copies in quad:
+        for copy in copies:
+            copy.wait_send()
     store.wait()
 
 
@@ -387,8 +388,8 @@
             dma((leaves - 1,)),
             dma((4,)),
             dma((4,)),
-            dma((3,)),
-            dma((3,)),
+            dma((6,)),
+            dma((6,)),
             dma((3,)),
             dma((sparse.shape[0],)),
         ],
@@ -474,8 +475,8 @@
                 work[b][base + end : base + S, :] = old - product[:, b * BLK : (b + 1) * BLK]
 
 
-def factor_kernel(gram_ref, samples_ref, row_ref, col_ref, transfer_ref, w0, w1):
-    work = (w0, w1)
+def load_grams(gram_ref, work):
+    w0, w1 = work
     corner_row = lax.broadcasted_iota(jnp.int32, (BLK, BLK), 0)
     corner_col = lax.broadcasted_iota(jnp.int32, (BLK, BLK), 1)
     for m in range(8):
@@ -490,32 +491,49 @@
             shared.T,
         )
         w0[at + BLK : at + S, :] = jnp.zeros((BLK, BLK), F32)
-    factorize(work, 6)
+
+
+def factor_kernel(gram_ref, samples_ref, row_ref, col_ref, transfer_ref, w0, w1):
+    work = (w0, w1)
+    step = pl.program_id(0)
+    width = row_ref.shape[1]
+
+    @pl.when(step == 0)
+    def _():
+        load_grams(gram_ref, work)
+        factorize(work, 6)
+
     row_id = lax.broadcasted_iota(jnp.int32, (S, S), 0)
     col_id = lax.broadcasted_iota(jnp.int32, (S, S), 1)
-
-    def read(m):
-        return jnp.concatenate(
-            [work[b][m * PITCH : m * PITCH + S, :] for b in range(2)], axis=1
-        )
-
-    gain = math.sqrt(samples_ref.shape[2])
+    gain = math.sqrt(2 * width)
+
+    def read(level, k):
+        at = (2 * level + k) * PITCH
+        return jnp.concatenate([work[b][at : at + S, :] for b in range(2)], axis=1)
+
+    def inverse(level, k):
+        return jnp.where(col_id <= row_id, read(level, k), 0.0)
+
+    def upper(level, k):
+        x = read(level, k)
+        return jnp.where(col_id > row_id, x, jnp.where(col_id == row_id, 1.0 / x, 0.0))
+
     for k in range(2):
-        found = [read(2 * level + k) for level in range(3)]
-        inverse = [jnp.where(col_id <= row_id, x, 0.0) for x in found]
-        upper = [
-            jnp.where(col_id > row_id, x, jnp.where(col_id == row_id, 1.0 / x, 0.0))
-            for x in found[:2]
-        ]
-        basis = dot3(inverse[0], samples_ref[k], ((1,), (0,))) * gain
-        (row_ref, col_ref)[k][...] = basis.astype(BF16)
-        for level in range(2):
-            transfer_ref[k, level] = dot3(upper[level], inverse[level + 1], ((1,), (1,)))
+        for part in range(2):
+
+            @pl.when(step == 1 + 2 * k + part)
+            def _():
+                basis = dot3(inverse(0, k), samples_ref[0], ((1,), (0,))) * gain
+                (row_ref, col_ref)[k][...] = basis.astype(BF16)
+                transfer_ref[0, part] = dot3(upper(part, k), inverse(part + 1, k), ((1,), (1,)))
+
+
+def later(step, start):
+    return jnp.maximum(step - start, 0)
 
 
 def factor(grams, samples):
     rows = samples.shape[2]
-    vmem = pl.BlockSpec(memory_space=pltpu.VMEM)
     return pl.pallas_call(
         factor_kernel,
         out_shape=[
@@ -523,8 +541,16 @@
             jax.ShapeDtypeStruct((S, rows), BF16),
             jax.ShapeDtypeStruct((2, 2, S, S), F32),
         ],
-        in_specs=[vmem] * 2,
-        out_specs=[vmem] * 3,
+        grid=(5,),
+        in_specs=[
+            pl.BlockSpec(grams.shape, lambda i: (0, 0, 0, 0)),
+            pl.BlockSpec((1, S, rows // 2), lambda i: (later(i, 1) // 2, 0, later(i, 1) % 2)),
+        ],
+        out_specs=[
+            pl.BlockSpec((S, rows // 2), lambda i: (0, jnp.minimum(later(i, 1), 1))),
+            pl.BlockSpec((S, rows // 2), lambda i: (0, jnp.minimum(later(i, 3), 1))),
+            pl.BlockSpec((1, 2, S, S), lambda i: (later(i, 1) // 2, 0, 0, 0)),
+        ],
         scratch_shapes=[pltpu.VMEM((8 * PITCH, BLK), F32)] * 2,
         compiler_params=params(),
         name="factor",
@@ -535,13 +561,11 @@
     child_samples, child_map, forward_probe, adjoint_probe, stored_sparse_blocks, block_pattern
 ):
     leaves = lax.axis_size("col")
-    row_pos = lax.axis_index("row")
-    pattern = lax.dynamic_index_in_dim(block_pattern, row_pos, 0, keepdims=False)
     sent, above, own, below, blocked = local_terms(
-        pattern, child_map, adjoint_probe, forward_probe, stored_sparse_blocks, child_samples, leaves
+        block_pattern, child_map, adjoint_probe, forward_probe, stored_sparse_blocks, child_samples, leaves
     )
     samples, grams = exchange(
-        pattern, blocked, sent, above, own, below, stored_sparse_blocks
+        block_pattern, blocked, sent, above, own, below, stored_sparse_blocks
     )
     return tuple(factor(grams, samples))
 

time: 62.8 us -> 63.9 us (1.018)
  Pallas kernels: 60.4 us -> 62.8 us
  local copies, waits for them, and re-layouts: 1.42 us -> 0 us
    pallas_call x1, Pallas kernels: 15.4 us -> 16.9 us  [factor(): pl.pallas_call(factor_kernel, out_shape=[jax.ShapeDtypeStruct((S, rows),...]
    unnamed x2 -> x0, local copies, waits for them, and re-layouts: 0.83 us -> none
    pallas_call x1, Pallas kernels: 10 us -> 10.9 us  [local_terms(): pl.pallas_call(terms_kernel, grid=(blocks,), out_shape=[jax.ShapeDtypeStr...]
where the time goes in v4:
time: 63.9 us; the launch traced here: 63.5 us
  Pallas kernels  62.8 us (98%)
  between operations  0.65 us (1%)
    pallas_call x1, Pallas kernels, exchange(): pl.pallas_call(exchange_kernel, out_shape=[jax.ShapeDtypeStruct((2, S, ro...  35.1 us
    pallas_call x1, Pallas kernels, factor(): pl.pallas_call(factor_kernel, out_shape=[jax.ShapeDtypeStruct((S, rows),...  16.9 us
    pallas_call x1, Pallas kernels, local_terms(): pl.pallas_call(terms_kernel, grid=(blocks,), out_shape=[jax.ShapeDtypeStr...  10.9 us

profile of v4, /device:TPU:96, one launch (start us, length us, event | category | flops | bytes accessed | tf_op | source)
XLA Modules:
  0.0 63.5 jit_solution(14650606921218994052)
XLA Ops:
  0.6 10.9 %terms.1 = (bf16[16,2,16,1024]{3,2,1,0:T(8,128)(2,1)}, bf16[8,256,128]{2,1,0:T(8,128)(2,1)}, f32[8,256,128]{2,1,0:T(8,128)}, bf16[8,256,128]{2,1,0:T(8,128)(2,1)}, bf16[8,256,128]{2,1,0:T(8,128)(2,1)}) custom-call(s32[16,8,18]{2,1,0:T(8,128)} %pattern_ref.3, s32[2,128]{1,0:T(2,128)} %map_ref.1, bf16[256,1024]{1,0:T(8,128)(2,1)} %probe_ref.1, ...), custom_call_target="tpu_custom_call" | custom-call | tf_op jit(solution)/shard_map/terms/pallas_call | solution.py:110
  11.5 35.1 %exchange.1 = (f32[2,256,1024]{2,1,0:T(8,128)}, f32[3,2,272,128]{3,2,1,0:T(8,128)}) custom-call(s32[16,8,18]{2,1,0:T(8,128)} %pattern_ref.3, bf16[8,256,128]{2,1,0:T(8,128)(2,1)} %get-tuple-element.10.probe_ref, bf16[16,2,16,1024]{3,2,1,0:T(8,128)(2,1)} %get-tuple-element.11.sent_ref, bf16[8,256,128]{2,1,0:T(8,128)(2,1)} %get-tuple-element.12.above_ref, ...), custom_call_target="tpu_custom_call" | custom-call | tf_op jit(solution)/shard_map/exchange/pallas_call | solution.py:367
  46.6 16.9 %factor.1 = (bf16[256,1024]{1,0:T(8,128)(2,1)}, bf16[256,1024]{1,0:T(8,128)(2,1)}, f32[2,2,256,256]{3,2,1,0:T(8,128)}) custom-call(f32[3,2,272,128]{3,2,1,0:T(8,128)} %get-tuple-element.15.gram_ref, f32[2,256,1024]{2,1,0:T(8,128)} %get-tuple-element.16.samples_ref), custom_call_target="tpu_custom_call" | custom-call | tf_op jit(solution)/shard_map/factor/pallas_call | solution.py:537

commit v5 on v4

--- a/solution.py
+++ b/solution.py
@@ -41,103 +41,69 @@
     return out
 
 
-def terms_kernel(
-    pattern_ref, map_ref, probe_ref, forward_ref, sparse_ref, child_ref,
-    sent_ref, above_ref, own_ref, below_ref, blocked_ref,
-    acc0, acc1, acc2, child, child_sem,
+def extend_kernel(
+    map_ref, pattern_ref, child_ref, forward_ref, sent_ref, blocked_ref, prior_ref, final_ref
 ):
-    b = pl.program_id(0)
-    steps = pl.num_programs(0)
     row = lax.axis_index("row")
-    accs = (acc0, acc1, acc2)
-    fetch = pltpu.make_async_copy(child_ref, child, child_sem)
-
-    @pl.when(b == 0)
-    def _():
-        fetch.start()
-        for acc in accs:
-            acc[...] = jnp.zeros_like(acc)
-
-    blocked_ref[0] = forward_ref[...]
-    probe = probe_ref[...]
-    for s in range(0, SLOTS, 2):
-        for q in range(3):
-            slot = q * SLOTS + s
-            pair = jnp.concatenate([sparse_ref[0, slot], sparse_ref[0, slot + 1]], axis=1)
-            product = jnp.dot(probe, pair, preferred_element_type=F32)
-            for i in range(2):
-                target = pattern_ref[row, b, slot + i]
-                accs[q][target] += product[:, i * BLK : (i + 1) * BLK]
-
     leaves = sent_ref.shape[0]
-    blocks = sent_ref.shape[3] // BLK
-    first_step = 4
-    share = leaves // 4
-
-    @pl.when(b == first_step)
-    def _():
-        fetch.wait()
-
-    @pl.when(b >= first_step)
-    def _():
-        def leaf(i, carry):
-            d = (b - first_step) * share + i
-            for c in range(blocks):
-                first = pl.multiple_of(map_ref[0, d * blocks + c] * BLK, BLK)
-                second = pl.multiple_of(map_ref[1, d * blocks + c] * BLK, BLK)
-                for k in range(2):
-                    x = child[0, k, :, pl.ds(first, BLK)].astype(F32)
-                    y = child[1, k, :, pl.ds(second, BLK)].astype(F32)
-                    sent_ref[d, k, :, c * BLK : (c + 1) * BLK] = (x + y).astype(BF16)
-            return carry
-
-        lax.fori_loop(0, share, leaf, 0)
-
-    @pl.when(b == steps - 1)
-    def _():
-        above_ref[...] = acc0[...].astype(BF16)
-        own_ref[...] = acc1[...]
-        below_ref[...] = acc2[...].astype(BF16)
-
-
-def local_terms(pattern, child_map, probe, forward_probe, sparse, child_samples, leaves):
-    blocks = sparse.shape[0]
+    blocks = blocked_ref.shape[0]
+    none = blocks * SLOTS
+    for q in range(3):
+        for c in range(blocks):
+            final_ref[q, c] = none
+    for b in range(blocks):
+        blocked_ref[b] = forward_ref[:, b * BLK : (b + 1) * BLK]
+
+    def link(b, s):
+        q = s // SLOTS
+        target = pattern_ref[row, b, s]
+        prior_ref[b, s] = final_ref[q, target]
+        final_ref[q, target] = b * SLOTS + s - q * SLOTS
+
+    def leaf(d, carry):
+        for c in range(blocks):
+            first = pl.multiple_of(map_ref[0, d * blocks + c] * BLK, BLK)
+            second = pl.multiple_of(map_ref[1, d * blocks + c] * BLK, BLK)
+            for k in range(2):
+                x = child_ref[0, k, :, pl.ds(first, BLK)].astype(F32)
+                y = child_ref[1, k, :, pl.ds(second, BLK)].astype(F32)
+                sent_ref[d, k, :, c * BLK : (c + 1) * BLK] = (x + y).astype(BF16)
+        return carry
+
+    def linked_leaf(d, carry):
+        for s in range(3 * SLOTS):
+            link(d, s)
+        return leaf(d, carry)
+
+    lax.fori_loop(0, blocks, linked_leaf, 0)
+    lax.fori_loop(blocks, leaves, leaf, 0)
+
+
+def extend(child_map, pattern, child_samples, forward_probe, leaves):
     samples_here, rows_group = child_samples.shape[2:]
-    shape = (blocks, S, BLK)
-    sent = (leaves, 2, samples_here, rows_group // leaves)
-    whole = pl.BlockSpec(shape, lambda b: (0, 0, 0))
+    rows = forward_probe.shape[1]
+    blocks = rows // BLK
     smem = pl.BlockSpec(memory_space=pltpu.SMEM)
+    vmem = pl.BlockSpec(memory_space=pltpu.VMEM)
     return pl.pallas_call(
-        terms_kernel,
-        grid=(blocks,),
+        extend_kernel,
         out_shape=[
-            jax.ShapeDtypeStruct(sent, BF16),
-            jax.ShapeDtypeStruct(shape, BF16),
-            jax.ShapeDtypeStruct(shape, F32),
-            jax.ShapeDtypeStruct(shape, BF16),
-            jax.ShapeDtypeStruct(shape, BF16),
+            jax.ShapeDtypeStruct((leaves, 2, samples_here, rows_group // leaves), BF16),
+            jax.ShapeDtypeStruct((blocks, S, BLK), BF16),
+            jax.ShapeDtypeStruct((blocks, 3 * SLOTS), jnp.int32),
+            jax.ShapeDtypeStruct((3, blocks), jnp.int32),
         ],
-        in_specs=[
-            smem,
-            smem,
-            pl.BlockSpec((S, BLK), lambda b: (0, b)),
-            pl.BlockSpec((S, BLK), lambda b: (0, b)),
-            pl.BlockSpec((1, 3 * SLOTS, BLK, BLK), lambda b: (b, 0, 0, 0)),
-            pl.BlockSpec(memory_space=pl.ANY),
-        ],
-        out_specs=[pl.BlockSpec(sent, lambda b: (0, 0, 0, 0)), whole, whole, whole]
-        + [pl.BlockSpec((1, S, BLK), lambda b: (b, 0, 0))],
-        scratch_shapes=[pltpu.VMEM(shape, F32)] * 3
-        + [pltpu.VMEM(child_samples.shape, BF16), pltpu.SemaphoreType.DMA],
+        in_specs=[smem, smem, vmem, vmem],
+        out_specs=[vmem, vmem, smem, smem],
         compiler_params=params(),
-        name="terms",
-    )(pattern, child_map, probe, forward_probe, sparse, child_samples)
+        name="extend",
+    )(child_map, pattern, child_samples, forward_probe)
 
 
 def exchange_kernel(
-    pattern_ref, probe_ref, sent_ref, above_ref, own_ref, below_ref, sparse_ref,
+    pattern_ref, prior_ref, final_ref, probe_ref, adjoint_ref, sent_ref, sparse_ref,
     samples_ref, gram_ref,
-    ext, before, after, down, up, own, blocks, samples, gram, packed, partner,
+    ext, before, after, down, up, above, below, sums, blocks, samples, gram, packed, partner,
     ext_send, ext_recv, row_send, row_recv, quad_send, quad_recv, local_sem, block_sem,
 ):
     row = lax.axis_index("row")
@@ -168,11 +134,9 @@
         pltpu.make_async_copy(sparse_ref.at[b], blocks.at[b], block_sem.at[b])
         for b in range(n_blocks)
     ]
-    own_fetch = pltpu.make_async_copy(own_ref, own, local_sem.at[0])
     ext_fetch = pltpu.make_async_copy(sent_ref.at[col], ext.at[col], local_sem.at[1])
     for fetch in fetches:
         fetch.start()
-    own_fetch.start()
     ext_fetch.start()
 
     @pl.when(row == 0)
@@ -195,8 +159,8 @@
             device_id_type=MESH,
         )
 
-    rising = [to_row(probe_ref, before, 0, 1), to_row(below_ref, up, 1, 1)]
-    falling = [to_row(probe_ref, after, 2, -1), to_row(above_ref, down, 3, -1)]
+    rising = [to_row(probe_ref, before, 0, 1), to_row(below, up, 1, 1)]
+    falling = [to_row(probe_ref, after, 2, -1), to_row(above, down, 3, -1)]
 
     pl.semaphore_wait(barrier, n_col + 1)
 
@@ -236,8 +200,47 @@
             preferred_element_type=F32,
         )
 
+    none = n_blocks * SLOTS
+    for q in range(3):
+        sums[q, none] = jnp.zeros((S, BLK), F32)
     for fetch in fetches:
         fetch.wait()
+
+    def adjoint_regions(regions):
+        def step(b, carry):
+            probe = adjoint_ref[:, pl.ds(pl.multiple_of(b * BLK, BLK), BLK)]
+            for s in range(0, SLOTS, 2):
+                for q in regions:
+                    slot = q * SLOTS + s
+                    pair = jnp.concatenate([blocks[b, slot], blocks[b, slot + 1]], axis=1)
+                    product = jnp.dot(probe, pair, preferred_element_type=F32)
+                    for i in range(2):
+                        sums[q, b * SLOTS + s + i] = (
+                            product[:, i * BLK : (i + 1) * BLK]
+                            + sums[q, prior_ref[b, slot + i]]
+                        )
+            return carry
+
+        lax.fori_loop(0, n_blocks, step, 0)
+
+    adjoint_regions((0, 2))
+
+    def settle(c, carry):
+        above[c] = sums[0, final_ref[0, c]].astype(BF16)
+        below[c] = sums[2, final_ref[2, c]].astype(BF16)
+        return carry
+
+    lax.fori_loop(0, n_blocks, settle, 0)
+
+    @pl.when(inner_up)
+    def _():
+        rising[1].start()
+
+    @pl.when(inner_down)
+    def _():
+        falling[1].start()
+
+    adjoint_regions((1,))
 
     def own_region(b, carry):
         lanes = pl.ds(pl.multiple_of(b * BLK, BLK), BLK)
@@ -253,14 +256,6 @@
     @pl.when(inner_up)
     def _():
         falling[0].wait_recv()
-
-    @pl.when(inner_up)
-    def _():
-        rising[1].start()
-
-    @pl.when(inner_down)
-    def _():
-        falling[1].start()
 
     def other_regions(b, carry):
         lanes = pl.ds(pl.multiple_of(b * BLK, BLK), BLK)
@@ -312,7 +307,6 @@
     for copy in spread:
         copy.wait_recv()
     finish(0, lambda h, lanes: samples[0, :, lanes])
-    own_fetch.wait()
 
     @pl.when(inner_down)
     def _():
@@ -326,7 +320,7 @@
         parts = []
         for c in range(2):
             at = h * 2 + c
-            parts.append(own[at] + down[at].astype(F32) + up[at].astype(F32))
+            parts.append(sums[1, final_ref[1, at]] + down[at].astype(F32) + up[at].astype(F32))
         return jnp.concatenate(parts, axis=1)
 
     finish(1, adjoint_terms)
@@ -357,7 +351,7 @@
     store.wait()
 
 
-def exchange(pattern, probe, sent, above, own, below, sparse):
+def exchange(pattern, prior, final, probe, adjoint_probe, sent, sparse):
     rows = sent.shape[3]
     leaves = sent.shape[0]
     held = 2 * BLK + 16
@@ -370,15 +364,17 @@
             jax.ShapeDtypeStruct((2, S, rows), F32),
             jax.ShapeDtypeStruct((3, 2, held, BLK), F32),
         ],
-        in_specs=[pl.BlockSpec(memory_space=pltpu.SMEM), vmem] + [anywhere] * 5,
+        in_specs=[pl.BlockSpec(memory_space=pltpu.SMEM)] * 3 + [vmem] * 2 + [anywhere] * 2,
         out_specs=[anywhere, vmem],
         scratch_shapes=[
             pltpu.VMEM(sent.shape, BF16),
             pltpu.VMEM(probe.shape, BF16),
             pltpu.VMEM(probe.shape, BF16),
-            pltpu.VMEM(above.shape, BF16),
-            pltpu.VMEM(below.shape, BF16),
-            pltpu.VMEM(own.shape, F32),
+            pltpu.VMEM(probe.shape, BF16),
+            pltpu.VMEM(probe.shape, BF16),
+            pltpu.VMEM(probe.shape, BF16),
+            pltpu.VMEM(probe.shape, BF16),
+            pltpu.VMEM((3, sparse.shape[0] * SLOTS + 1, S, BLK), F32),
             pltpu.VMEM(sparse.shape, BF16),
             pltpu.VMEM((2, S, rows), F32),
             pltpu.VMEM((2, S, S), F32),
@@ -397,7 +393,7 @@
             collective_id=0, has_side_effects=True, vmem_limit_bytes=VMEM_LIMIT
         ),
         name="exchange",
-    )(pattern, probe, sent, above, own, below, sparse)
+    )(pattern, prior, final, probe, adjoint_probe, sent, sparse)
 
 
 def splat(x, at):
@@ -495,45 +491,30 @@
 
 def factor_kernel(gram_ref, samples_ref, row_ref, col_ref, transfer_ref, w0, w1):
     work = (w0, w1)
-    step = pl.program_id(0)
-    width = row_ref.shape[1]
-
-    @pl.when(step == 0)
-    def _():
-        load_grams(gram_ref, work)
-        factorize(work, 6)
-
+    load_grams(gram_ref, work)
+    factorize(work, 6)
     row_id = lax.broadcasted_iota(jnp.int32, (S, S), 0)
     col_id = lax.broadcasted_iota(jnp.int32, (S, S), 1)
-    gain = math.sqrt(2 * width)
-
-    def read(level, k):
-        at = (2 * level + k) * PITCH
-        return jnp.concatenate([work[b][at : at + S, :] for b in range(2)], axis=1)
-
-    def inverse(level, k):
-        return jnp.where(col_id <= row_id, read(level, k), 0.0)
-
-    def upper(level, k):
-        x = read(level, k)
-        return jnp.where(col_id > row_id, x, jnp.where(col_id == row_id, 1.0 / x, 0.0))
-
+    gain = math.sqrt(samples_ref.shape[2])
     for k in range(2):
-        for part in range(2):
-
-            @pl.when(step == 1 + 2 * k + part)
-            def _():
-                basis = dot3(inverse(0, k), samples_ref[0], ((1,), (0,))) * gain
-                (row_ref, col_ref)[k][...] = basis.astype(BF16)
-                transfer_ref[0, part] = dot3(upper(part, k), inverse(part + 1, k), ((1,), (1,)))
-
-
-def later(step, start):
-    return jnp.maximum(step - start, 0)
+        found = []
+        for level in range(3):
+            at = (2 * level + k) * PITCH
+            found.append(jnp.concatenate([work[b][at : at + S, :] for b in range(2)], axis=1))
+        inverse = [jnp.where(col_id <= row_id, x, 0.0) for x in found]
+        upper = [
+            jnp.where(col_id > row_id, x, jnp.where(col_id == row_id, 1.0 / x, 0.0))
+            for x in found[:2]
+        ]
+        basis = dot3(inverse[0], samples_ref[k], ((1,), (0,))) * gain
+        (row_ref, col_ref)[k][...] = basis.astype(BF16)
+        for level in range(2):
+            transfer_ref[k, level] = dot3(upper[level], inverse[level + 1], ((1,), (1,)))
 
 
 def factor(grams, samples):
     rows = samples.shape[2]
+    vmem = pl.BlockSpec(memory_space=pltpu.VMEM)
     return pl.pallas_call(
         factor_kernel,
         out_shape=[
@@ -541,16 +522,8 @@
             jax.ShapeDtypeStruct((S, rows), BF16),
             jax.ShapeDtypeStruct((2, 2, S, S), F32),
         ],
-        grid=(5,),
-        in_specs=[
-            pl.BlockSpec(grams.shape, lambda i: (0, 0, 0, 0)),
-            pl.BlockSpec((1, S, rows // 2), lambda i: (later(i, 1) // 2, 0, later(i, 1) % 2)),
-        ],
-        out_specs=[
-            pl.BlockSpec((S, rows // 2), lambda i: (0, jnp.minimum(later(i, 1), 1))),
-            pl.BlockSpec((S, rows // 2), lambda i: (0, jnp.minimum(later(i, 3), 1))),
-            pl.BlockSpec((1, 2, S, S), lambda i: (later(i, 1) // 2, 0, 0, 0)),
-        ],
+        in_specs=[vmem] * 2,
+        out_specs=[vmem] * 3,
         scratch_shapes=[pltpu.VMEM((8 * PITCH, BLK), F32)] * 2,
         compiler_params=params(),
         name="factor",
@@ -561,11 +534,11 @@
     child_samples, child_map, forward_probe, adjoint_probe, stored_sparse_blocks, block_pattern
 ):
     leaves = lax.axis_size("col")
-    sent, above, own, below, blocked = local_terms(
-        block_pattern, child_map, adjoint_probe, forward_probe, stored_sparse_blocks, child_samples, leaves
+    sent, blocked, prior, final = extend(
+        child_map, block_pattern, child_samples, forward_probe, leaves
     )
     samples, grams = exchange(
-        block_pattern, blocked, sent, above, own, below, stored_sparse_blocks
+        block_pattern, prior, final, blocked, adjoint_probe, sent, stored_sparse_blocks
     )
     return tuple(factor(grams, samples))
 

time: 63.9 us -> 55.6 us (0.87)
  Pallas kernels: 62.8 us -> 54.8 us
    pallas_call x1, Pallas kernels: 10.9 us -> 4.21 us  [extend(): pl.pallas_call(extend_kernel, out_shape=[jax.ShapeDtypeStruct((leaves, 2,...]
    pallas_call x1, Pallas kernels: 16.9 us -> 15.4 us  [factor(): pl.pallas_call(factor_kernel, out_shape=[jax.ShapeDtypeStruct((S, rows),...]
where the time goes in v5:
time: 55.6 us; the launch traced here: 55.4 us
  Pallas kernels  54.8 us (99%)
  between operations  0.65 us (1%)
    pallas_call x1, Pallas kernels, exchange(): pl.pallas_call(exchange_kernel, out_shape=[jax.ShapeDtypeStruct((2, S, ro...  35.2 us
    pallas_call x1, Pallas kernels, factor(): pl.pallas_call(factor_kernel, out_shape=[jax.ShapeDtypeStruct((S, rows),...  15.4 us
    pallas_call x1, Pallas kernels, extend(): pl.pallas_call(extend_kernel, out_shape=[jax.ShapeDtypeStruct((leaves, 2,...  4.21 us

profile of v5, /device:TPU:96, one launch (start us, length us, event | category | flops | bytes accessed | tf_op | source)
XLA Modules:
  0.0 55.4 jit_solution(6829178950143574980)
XLA Ops:
  0.6 4.2 %extend.1 = (bf16[16,2,16,1024]{3,2,1,0:T(8,128)(2,1)}, bf16[8,256,128]{2,1,0:T(8,128)(2,1)}, s32[8,18]{1,0:T(8,128)}, s32[3,8]{1,0:T(4,128)}) custom-call(s32[2,128]{1,0:T(2,128)} %map_ref.1, s32[16,8,18]{2,1,0:T(8,128)} %pattern_ref.3, bf16[2,2,16,16384]{3,2,1,0:T(8,128)(2,1)} %child_ref.1, bf16[256,1024]{1,0:T(8,128)(2,1)} %forward_ref.1), custom_call_target="tpu_custom_call" | custom-call | tf_op jit(solution)/shard_map/extend/pallas_call | solution.py:88
  4.8 35.2 %exchange.1 = (f32[2,256,1024]{2,1,0:T(8,128)}, f32[3,2,272,128]{3,2,1,0:T(8,128)}) custom-call(s32[16,8,18]{2,1,0:T(8,128)} %pattern_ref.3, s32[8,18]{1,0:T(8,128)} %get-tuple-element.9.prior_ref, s32[3,8]{1,0:T(4,128)} %get-tuple-element.10.final_ref, bf16[8,256,128]{2,1,0:T(8,128)(2,1)} %get-tuple-element.11.probe_ref, bf16[256,1024]{1,0:T(8,128)(2,1)} %adjoint_ref.1, ...), custom_call_target="tpu_custom_call" | custom-call | tf_op jit(solution)/shard_map/exchange/pallas_call | solution.py:361
  40.0 15.4 %factor.1 = (bf16[256,1024]{1,0:T(8,128)(2,1)}, bf16[256,1024]{1,0:T(8,128)(2,1)}, f32[2,2,256,256]{3,2,1,0:T(8,128)}) custom-call(f32[3,2,272,128]{3,2,1,0:T(8,128)} %get-tuple-element.13.gram_ref, f32[2,256,1024]{2,1,0:T(8,128)} %get-tuple-element.14.samples_ref), custom_call_target="tpu_custom_call" | custom-call | tf_op jit(solution)/shard_map/factor/pallas_call | solution.py:518

commit v6 on v5

--- a/solution.py
+++ b/solution.py
@@ -162,6 +162,30 @@
     rising = [to_row(probe_ref, before, 0, 1), to_row(below, up, 1, 1)]
     falling = [to_row(probe_ref, after, 2, -1), to_row(above, down, 3, -1)]
 
+    none = n_blocks * SLOTS
+    for q in range(3):
+        sums[q, none] = jnp.zeros((S, BLK), F32)
+    def adjoint_regions(regions, begin, end):
+        def step(b, carry):
+            probe = adjoint_ref[:, pl.ds(pl.multiple_of(b * BLK, BLK), BLK)]
+            for s in range(0, SLOTS, 2):
+                for q in regions:
+                    slot = q * SLOTS + s
+                    pair = jnp.concatenate([blocks[b, slot], blocks[b, slot + 1]], axis=1)
+                    product = jnp.dot(probe, pair, preferred_element_type=F32)
+                    for i in range(2):
+                        sums[q, b * SLOTS + s + i] = (
+                            product[:, i * BLK : (i + 1) * BLK]
+                            + sums[q, prior_ref[b, slot + i]]
+                        )
+            return carry
+
+        lax.fori_loop(begin, end, step, 0)
+
+    early = n_blocks // 2
+    for fetch in fetches[:early]:
+        fetch.wait()
+    adjoint_regions((0, 2), 0, early)
     pl.semaphore_wait(barrier, n_col + 1)
 
     @pl.when(inner_up)
@@ -174,13 +198,14 @@
 
     spread = [
         pltpu.make_async_remote_copy(
-            src_ref=sent_ref.at[peer],
-            dst_ref=ext.at[col],
-            send_sem=ext_send.at[i],
-            recv_sem=ext_recv.at[i],
+            src_ref=sent_ref.at[peer, k],
+            dst_ref=ext.at[col, k],
+            send_sem=ext_send.at[k, i],
+            recv_sem=ext_recv.at[k, i],
             device_id=(row, peer),
             device_id_type=MESH,
         )
+        for k in range(2)
         for i, peer in enumerate(peers)
     ]
     for copy in spread:
@@ -200,30 +225,9 @@
             preferred_element_type=F32,
         )
 
-    none = n_blocks * SLOTS
-    for q in range(3):
-        sums[q, none] = jnp.zeros((S, BLK), F32)
-    for fetch in fetches:
+    for fetch in fetches[early:]:
         fetch.wait()
-
-    def adjoint_regions(regions):
-        def step(b, carry):
-            probe = adjoint_ref[:, pl.ds(pl.multiple_of(b * BLK, BLK), BLK)]
-            for s in range(0, SLOTS, 2):
-                for q in regions:
-                    slot = q * SLOTS + s
-                    pair = jnp.concatenate([blocks[b, slot], blocks[b, slot + 1]], axis=1)
-                    product = jnp.dot(probe, pair, preferred_element_type=F32)
-                    for i in range(2):
-                        sums[q, b * SLOTS + s + i] = (
-                            product[:, i * BLK : (i + 1) * BLK]
-                            + sums[q, prior_ref[b, slot + i]]
-                        )
-            return carry
-
-        lax.fori_loop(0, n_blocks, step, 0)
-
-    adjoint_regions((0, 2))
+    adjoint_regions((0, 2), early, n_blocks)
 
     def settle(c, carry):
         above[c] = sums[0, final_ref[0, c]].astype(BF16)
@@ -239,8 +243,6 @@
     @pl.when(inner_down)
     def _():
         falling[1].start()
-
-    adjoint_regions((1,))
 
     def own_region(b, carry):
         lanes = pl.ds(pl.multiple_of(b * BLK, BLK), BLK)
@@ -304,9 +306,12 @@
         quad.append(copies)
 
     ext_fetch.wait()
-    for copy in spread:
+    for copy in spread[: n_col - 1]:
         copy.wait_recv()
     finish(0, lambda h, lanes: samples[0, :, lanes])
+    adjoint_regions((1,), 0, n_blocks)
+    for copy in spread[n_col - 1 :]:
+        copy.wait_recv()
 
     @pl.when(inner_down)
     def _():
@@ -380,8 +385,8 @@
             pltpu.VMEM((2, S, S), F32),
             pltpu.VMEM((2, held, BLK), BF16),
             pltpu.VMEM((3, 2, held, BLK), BF16),
-            dma((leaves - 1,)),
-            dma((leaves - 1,)),
+            dma((2, leaves - 1)),
+            dma((2, leaves - 1)),
             dma((4,)),
             dma((4,)),
             dma((6,)),

time: 55.6 us -> 52.9 us (0.951); the launches traced: 55.4 us -> 52 us
  Pallas kernels: 54.8 us -> 51.4 us
    pallas_call x1, Pallas kernels: 35.2 us -> 31.8 us  [exchange(): pl.pallas_call(exchange_kernel, out_shape=[jax.ShapeDtypeStruct((2, S, ro...]
where the time goes in v6:
time: 52.9 us; the launch traced here: 52 us
  Pallas kernels  51.4 us (97%)
  between operations  0.65 us (1%)
    pallas_call x1, Pallas kernels, exchange(): pl.pallas_call(exchange_kernel, out_shape=[jax.ShapeDtypeStruct((2, S, ro...  31.8 us
    pallas_call x1, Pallas kernels, factor(): pl.pallas_call(factor_kernel, out_shape=[jax.ShapeDtypeStruct((S, rows),...  15.4 us
    pallas_call x1, Pallas kernels, extend(): pl.pallas_call(extend_kernel, out_shape=[jax.ShapeDtypeStruct((leaves, 2,...  4.21 us

profile of v6, /device:TPU:96, one launch (start us, length us, event | category | flops | bytes accessed | tf_op | source)
XLA Modules:
  0.0 52.0 jit_solution(16923370858052226849)
XLA Ops:
  0.6 4.2 %extend.1 = (bf16[16,2,16,1024]{3,2,1,0:T(8,128)(2,1)}, bf16[8,256,128]{2,1,0:T(8,128)(2,1)}, s32[8,18]{1,0:T(8,128)}, s32[3,8]{1,0:T(4,128)}) custom-call(s32[2,128]{1,0:T(2,128)} %map_ref.1, s32[16,8,18]{2,1,0:T(8,128)} %pattern_ref.3, bf16[2,2,16,16384]{3,2,1,0:T(8,128)(2,1)} %child_ref.1, bf16[256,1024]{1,0:T(8,128)(2,1)} %forward_ref.1), custom_call_target="tpu_custom_call" | custom-call | tf_op jit(solution)/shard_map/extend/pallas_call | solution.py:88
  4.8 31.8 %exchange.1 = (f32[2,256,1024]{2,1,0:T(8,128)}, f32[3,2,272,128]{3,2,1,0:T(8,128)}) custom-call(s32[16,8,18]{2,1,0:T(8,128)} %pattern_ref.3, s32[8,18]{1,0:T(8,128)} %get-tuple-element.9.prior_ref, s32[3,8]{1,0:T(4,128)} %get-tuple-element.10.final_ref, bf16[8,256,128]{2,1,0:T(8,128)(2,1)} %get-tuple-element.11.probe_ref, bf16[256,1024]{1,0:T(8,128)(2,1)} %adjoint_ref.1, ...), custom_call_target="tpu_custom_call" | custom-call | tf_op jit(solution)/shard_map/exchange/pallas_call | solution.py:366
  36.6 15.4 %factor.1 = (bf16[256,1024]{1,0:T(8,128)(2,1)}, bf16[256,1024]{1,0:T(8,128)(2,1)}, f32[2,2,256,256]{3,2,1,0:T(8,128)}) custom-call(f32[3,2,272,128]{3,2,1,0:T(8,128)} %get-tuple-element.13.gram_ref, f32[2,256,1024]{2,1,0:T(8,128)} %get-tuple-element.14.samples_ref), custom_call_target="tpu_custom_call" | custom-call | tf_op jit(solution)/shard_map/factor/pallas_call | solution.py:523

commit v7 on v6

--- a/solution.py
+++ b/solution.py
@@ -1,3 +1,4 @@
+from functools import partial
 import math
 
 import jax
@@ -182,7 +183,7 @@
 
         lax.fori_loop(begin, end, step, 0)
 
-    early = n_blocks // 2
+    early = 3 * n_blocks // 4
     for fetch in fetches[:early]:
         fetch.wait()
     adjoint_regions((0, 2), 0, early)
@@ -404,7 +405,7 @@
 def splat(x, at):
     return jnp.broadcast_to(x[:, at:at+1], (8, BLK))
 
-def eliminate(rows, first, half, lane):
+def eliminate(rows, first, half, lane, others):
     count=len(rows)
     for g in range(0, count, SUB):
         base=first+g
@@ -417,6 +418,10 @@
             for i in range(j+1,SUB):
                 for l in range(i,SUB):
                     e[i][l]=e[i][l]-f[i]*f[l]
+        share=-(-len(others)*SUB//(count-g))
+        for other in others[:share]:
+            other()
+        others=others[share:]
         clean=[]
         for j in range(SUB):
             here=lane==base+j
@@ -438,42 +443,58 @@
 
 def factorize(work, count):
     lane = lax.broadcasted_iota(jnp.int32, (8, BLK), 1)
+    others = []
     for lo in range(0, S, PANEL):
         half = lo // BLK
         rows = [
             [work[b][pl.ds(lo + i, 8, stride=PITCH), :] for b in range(2)] for i in range(PANEL)
         ]
-        rows = eliminate(rows, lo - half*BLK, half, lane)
+        rows = eliminate(rows, lo - half * BLK, half, lane, others)
         for i in range(PANEL):
             for b in range(2):
                 work[b][pl.ds(lo + i, 8, stride=PITCH), :] = rows[i][b]
         end = lo + PANEL
         if end == S:
             break
+        skip = end // BLK
         row_id = lax.broadcasted_iota(jnp.int32, (PANEL, BLK), 0) + lo
         col_id = lax.broadcasted_iota(jnp.int32, (PANEL, BLK), 1) + BLK * half
         dead = (col_id > row_id) & (col_id < end)
-        cols = lax.broadcasted_iota(jnp.int32, (S - end, BLK), 1) + BLK * half
-        mine = (cols >= lo) & (cols < end)
+        operands = []
         for m in range(count):
             base = m * PITCH
             panel = [work[b][base + lo : base + end, :] for b in range(2)]
             masked = [jnp.where(dead, 0.0, x) if b == half else x for b, x in enumerate(panel)]
-            skip = end // BLK
             left = panel[1] if skip else jnp.concatenate(panel, axis=1)
             lh, lm, ll = split3(left)
             rh, rm, rl = split3(jnp.concatenate(masked, axis=1))
-            product = lax.dot_general(
-                jnp.concatenate([lh, lh, lm, lh, ll, lm], axis=0),
-                jnp.concatenate([rh, rm, rh, rl, rh, rm], axis=0),
-                (((0,), (0,)), ((), ())),
-                preferred_element_type=F32,
-            )[end - skip * BLK :]
+            operands.append(
+                (
+                    jnp.concatenate([lh, lh, lm, lh, ll, lm], axis=0).T,
+                    jnp.concatenate([rh, rm, rh, rl, rh, rm], axis=0),
+                )
+            )
+
+        def update(m, begin, stop, lo=lo, end=end, half=half, skip=skip, operands=operands):
+            left, right = operands[m]
+            product = jnp.dot(
+                left[begin - skip * BLK : stop - skip * BLK], right, preferred_element_type=F32
+            )
+            cols = lax.broadcasted_iota(jnp.int32, (stop - begin, BLK), 1) + BLK * half
+            mine = (cols >= lo) & (cols < end)
+            base = m * PITCH
             for b in range(2):
-                old = work[b][base + end : base + S, :]
+                old = work[b][base + begin : base + stop, :]
                 if b == half:
                     old = jnp.where(mine, 0.0, old)
-                work[b][base + end : base + S, :] = old - product[:, b * BLK : (b + 1) * BLK]
+                work[b][base + begin : base + stop, :] = old - product[:, b * BLK : (b + 1) * BLK]
+
+        near = end + PANEL
+        for m in range(count):
+            update(m, end, near)
+        others = []
+        if near < S:
+            others = [partial(update, m, near, S) for m in range(count)]
 
 
 def load_grams(gram_ref, work):

time: 52.9 us -> 52.7 us (level)
    pallas_call x1, Pallas kernels: 31.8 us -> 33 us  [exchange(): pl.pallas_call(exchange_kernel, out_shape=[jax.ShapeDtypeStruct((2, S, ro...]
    pallas_call x1, Pallas kernels: 15.4 us -> 14.2 us  [factor(): pl.pallas_call(factor_kernel, out_shape=[jax.ShapeDtypeStruct((S, rows),...]
where the time goes in v7:
time: 52.7 us; the launch traced here: 52 us
  Pallas kernels  51.4 us (98%)
  between operations  0.65 us (1%)
    pallas_call x1, Pallas kernels, exchange(): pl.pallas_call(exchange_kernel, out_shape=[jax.ShapeDtypeStruct((2, S, ro...  33 us
    pallas_call x1, Pallas kernels, factor(): pl.pallas_call(factor_kernel, out_shape=[jax.ShapeDtypeStruct((S, rows),...  14.2 us
    pallas_call x1, Pallas kernels, extend(): pl.pallas_call(extend_kernel, out_shape=[jax.ShapeDtypeStruct((leaves, 2,...  4.21 us

profile of v7, /device:TPU:96, one launch (start us, length us, event | category | flops | bytes accessed | tf_op | source)
XLA Modules:
  0.0 52.0 jit_solution(4450935616654761306)
XLA Ops:
  0.6 4.2 %extend.1 = (bf16[16,2,16,1024]{3,2,1,0:T(8,128)(2,1)}, bf16[8,256,128]{2,1,0:T(8,128)(2,1)}, s32[8,18]{1,0:T(8,128)}, s32[3,8]{1,0:T(4,128)}) custom-call(s32[2,128]{1,0:T(2,128)} %map_ref.1, s32[16,8,18]{2,1,0:T(8,128)} %pattern_ref.3, bf16[2,2,16,16384]{3,2,1,0:T(8,128)(2,1)} %child_ref.1, bf16[256,1024]{1,0:T(8,128)(2,1)} %forward_ref.1), custom_call_target="tpu_custom_call" | custom-call | tf_op jit(solution)/shard_map/extend/pallas_call | solution.py:89
  4.8 33.0 %exchange.1 = (f32[2,256,1024]{2,1,0:T(8,128)}, f32[3,2,272,128]{3,2,1,0:T(8,128)}) custom-call(s32[16,8,18]{2,1,0:T(8,128)} %pattern_ref.3, s32[8,18]{1,0:T(8,128)} %get-tuple-element.9.prior_ref, s32[3,8]{1,0:T(4,128)} %get-tuple-element.10.final_ref, bf16[8,256,128]{2,1,0:T(8,128)(2,1)} %get-tuple-element.11.probe_ref, bf16[256,1024]{1,0:T(8,128)(2,1)} %adjoint_ref.1, ...), custom_call_target="tpu_custom_call" | custom-call | tf_op jit(solution)/shard_map/exchange/pallas_call | solution.py:367
  37.8 14.2 %factor.1 = (bf16[256,1024]{1,0:T(8,128)(2,1)}, bf16[256,1024]{1,0:T(8,128)(2,1)}, f32[2,2,256,256]{3,2,1,0:T(8,128)}) custom-call(f32[3,2,272,128]{3,2,1,0:T(8,128)} %get-tuple-element.13.gram_ref, f32[2,256,1024]{2,1,0:T(8,128)} %get-tuple-element.14.samples_ref), custom_call_target="tpu_custom_call" | custom-call | tf_op jit(solution)/shard_map/factor/pallas_call | solution.py:544

commit v8 on v7

--- a/solution.py
+++ b/solution.py
@@ -43,12 +43,18 @@
 
 
 def extend_kernel(
-    map_ref, pattern_ref, child_ref, forward_ref, sent_ref, blocked_ref, prior_ref, final_ref
+    map_ref, pattern_ref, child_ref, forward_ref, sent_ref, blocked_ref, prior_ref, final_ref,
+    child, child_sem,
 ):
     row = lax.axis_index("row")
     leaves = sent_ref.shape[0]
     blocks = blocked_ref.shape[0]
     none = blocks * SLOTS
+    fetches = [
+        pltpu.make_async_copy(child_ref.at[:, k], child.at[k], child_sem.at[k]) for k in range(2)
+    ]
+    for fetch in fetches:
+        fetch.start()
     for q in range(3):
         for c in range(blocks):
             final_ref[q, c] = none
@@ -61,23 +67,30 @@
         prior_ref[b, s] = final_ref[q, target]
         final_ref[q, target] = b * SLOTS + s - q * SLOTS
 
-    def leaf(d, carry):
+    def leaf(k, d):
         for c in range(blocks):
             first = pl.multiple_of(map_ref[0, d * blocks + c] * BLK, BLK)
             second = pl.multiple_of(map_ref[1, d * blocks + c] * BLK, BLK)
-            for k in range(2):
-                x = child_ref[0, k, :, pl.ds(first, BLK)].astype(F32)
-                y = child_ref[1, k, :, pl.ds(second, BLK)].astype(F32)
-                sent_ref[d, k, :, c * BLK : (c + 1) * BLK] = (x + y).astype(BF16)
+            x = child[k, 0, :, pl.ds(first, BLK)].astype(F32)
+            y = child[k, 1, :, pl.ds(second, BLK)].astype(F32)
+            sent_ref[d, k, :, c * BLK : (c + 1) * BLK] = (x + y).astype(BF16)
+
+    def first_half(i, carry):
+        for s in range(3 * SLOTS):
+            link(i, s)
+        for part in range(leaves // blocks):
+            leaf(0, i + part * blocks)
         return carry
 
-    def linked_leaf(d, carry):
-        for s in range(3 * SLOTS):
-            link(d, s)
-        return leaf(d, carry)
-
-    lax.fori_loop(0, blocks, linked_leaf, 0)
-    lax.fori_loop(blocks, leaves, leaf, 0)
+    def second_half(i, carry):
+        for part in range(leaves // blocks):
+            leaf(1, i + part * blocks)
+        return carry
+
+    fetches[0].wait()
+    lax.fori_loop(0, blocks, first_half, 0)
+    fetches[1].wait()
+    lax.fori_loop(0, blocks, second_half, 0)
 
 
 def extend(child_map, pattern, child_samples, forward_probe, leaves):
@@ -94,8 +107,12 @@
             jax.ShapeDtypeStruct((blocks, 3 * SLOTS), jnp.int32),
             jax.ShapeDtypeStruct((3, blocks), jnp.int32),
         ],
-        in_specs=[smem, smem, vmem, vmem],
+        in_specs=[smem, smem, pl.BlockSpec(memory_space=pl.ANY), vmem],
         out_specs=[vmem, vmem, smem, smem],
+        scratch_shapes=[
+            pltpu.VMEM(child_samples.shape, BF16),
+            pltpu.SemaphoreType.DMA((2,)),
+        ],
         compiler_params=params(),
         name="extend",
     )(child_map, pattern, child_samples, forward_probe)
@@ -183,7 +200,7 @@
 
         lax.fori_loop(begin, end, step, 0)
 
-    early = 3 * n_blocks // 4
+    early = n_blocks // 4
     for fetch in fetches[:early]:
         fetch.wait()
     adjoint_regions((0, 2), 0, early)

time: 52.7 us -> 53.6 us (1.017)
  the two profiles are of different devices: /device:TPU:96 before, /device:TPU:1 now
where the time goes in v8:
time: 53.6 us; the launch traced here: 53.3 us
  Pallas kernels  52.7 us (98%)
  between operations  0.65 us (1%)
    pallas_call x1, Pallas kernels, exchange(): pl.pallas_call(exchange_kernel, out_shape=[jax.ShapeDtypeStruct((2, S, ro...  32.7 us
    pallas_call x1, Pallas kernels, factor(): pl.pallas_call(factor_kernel, out_shape=[jax.ShapeDtypeStruct((S, rows),...  14.2 us
    pallas_call x1, Pallas kernels, extend(): pl.pallas_call(extend_kernel, out_shape=[jax.ShapeDtypeStruct((leaves, 2,...  5.78 us

profile of v8, /device:TPU:1, one launch (start us, length us, event | category | flops | bytes accessed | tf_op | source)
XLA Modules:
  0.0 53.3 jit_solution(7058035964090989662)
XLA Ops:
  0.6 5.8 %extend.1 = (bf16[16,2,16,1024]{3,2,1,0:T(8,128)(2,1)}, bf16[8,256,128]{2,1,0:T(8,128)(2,1)}, s32[8,18]{1,0:T(8,128)}, s32[3,8]{1,0:T(4,128)}) custom-call(s32[2,128]{1,0:T(2,128)} %map_ref.1, s32[16,8,18]{2,1,0:T(8,128)} %pattern_ref.3, bf16[2,2,16,16384]{3,2,1,0:T(8,128)(2,1)} %child_ref.1, bf16[256,1024]{1,0:T(8,128)(2,1)} %forward_ref.1), custom_call_target="tpu_custom_call" | custom-call | tf_op jit(solution)/shard_map/extend/pallas_call | solution.py:102
  6.4 32.7 %exchange.1 = (f32[2,256,1024]{2,1,0:T(8,128)}, f32[3,2,272,128]{3,2,1,0:T(8,128)}) custom-call(s32[16,8,18]{2,1,0:T(8,128)} %pattern_ref.3, s32[8,18]{1,0:T(8,128)} %get-tuple-element.9.prior_ref, s32[3,8]{1,0:T(4,128)} %get-tuple-element.10.final_ref, bf16[8,256,128]{2,1,0:T(8,128)(2,1)} %get-tuple-element.11.probe_ref, bf16[256,1024]{1,0:T(8,128)(2,1)} %adjoint_ref.1, ...), custom_call_target="tpu_custom_call" | custom-call | tf_op jit(solution)/shard_map/exchange/pallas_call | solution.py:384
  39.1 14.2 %factor.1 = (bf16[256,1024]{1,0:T(8,128)(2,1)}, bf16[256,1024]{1,0:T(8,128)(2,1)}, f32[2,2,256,256]{3,2,1,0:T(8,128)}) custom-call(f32[3,2,272,128]{3,2,1,0:T(8,128)} %get-tuple-element.13.gram_ref, f32[2,256,1024]{2,1,0:T(8,128)} %get-tuple-element.14.samples_ref), custom_call_target="tpu_custom_call" | custom-call | tf_op jit(solution)/shard_map/factor/pallas_call | solution.py:561

commit v9 on v7

--- a/solution.py
+++ b/solution.py
@@ -183,7 +183,7 @@
 
         lax.fori_loop(begin, end, step, 0)
 
-    early = 3 * n_blocks // 4
+    early = n_blocks // 2
     for fetch in fetches[:early]:
         fetch.wait()
     adjoint_regions((0, 2), 0, early)

time: 52.7 us -> 51.6 us (0.979)
  Pallas kernels: 51.4 us -> 50 us
    pallas_call x1, Pallas kernels: 33 us -> 31.6 us  [exchange(): pl.pallas_call(exchange_kernel, out_shape=[jax.ShapeDtypeStruct((2, S, ro...]
where the time goes in v9:
time: 51.6 us; the launch traced here: 50.6 us
  Pallas kernels  50 us (97%)
  between operations  0.65 us (1%)
    pallas_call x1, Pallas kernels, exchange(): pl.pallas_call(exchange_kernel, out_shape=[jax.ShapeDtypeStruct((2, S, ro...  31.6 us
    pallas_call x1, Pallas kernels, factor(): pl.pallas_call(factor_kernel, out_shape=[jax.ShapeDtypeStruct((S, rows),...  14.2 us
    pallas_call x1, Pallas kernels, extend(): pl.pallas_call(extend_kernel, out_shape=[jax.ShapeDtypeStruct((leaves, 2,...  4.21 us

profile of v9, /device:TPU:96, one launch (start us, length us, event | category | flops | bytes accessed | tf_op | source)
XLA Modules:
  0.0 50.6 jit_solution(7926887229277199084)
XLA Ops:
  0.6 4.2 %extend.1 = (bf16[16,2,16,1024]{3,2,1,0:T(8,128)(2,1)}, bf16[8,256,128]{2,1,0:T(8,128)(2,1)}, s32[8,18]{1,0:T(8,128)}, s32[3,8]{1,0:T(4,128)}) custom-call(s32[2,128]{1,0:T(2,128)} %map_ref.1, s32[16,8,18]{2,1,0:T(8,128)} %pattern_ref.3, bf16[2,2,16,16384]{3,2,1,0:T(8,128)(2,1)} %child_ref.1, bf16[256,1024]{1,0:T(8,128)(2,1)} %forward_ref.1), custom_call_target="tpu_custom_call" | custom-call | tf_op jit(solution)/shard_map/extend/pallas_call | solution.py:89
  4.8 31.6 %exchange.1 = (f32[2,256,1024]{2,1,0:T(8,128)}, f32[3,2,272,128]{3,2,1,0:T(8,128)}) custom-call(s32[16,8,18]{2,1,0:T(8,128)} %pattern_ref.3, s32[8,18]{1,0:T(8,128)} %get-tuple-element.9.prior_ref, s32[3,8]{1,0:T(4,128)} %get-tuple-element.10.final_ref, bf16[8,256,128]{2,1,0:T(8,128)(2,1)} %get-tuple-element.11.probe_ref, bf16[256,1024]{1,0:T(8,128)(2,1)} %adjoint_ref.1, ...), custom_call_target="tpu_custom_call" | custom-call | tf_op jit(solution)/shard_map/exchange/pallas_call | solution.py:367
  36.4 14.2 %factor.1 = (bf16[256,1024]{1,0:T(8,128)(2,1)}, bf16[256,1024]{1,0:T(8,128)(2,1)}, f32[2,2,256,256]{3,2,1,0:T(8,128)}) custom-call(f32[3,2,272,128]{3,2,1,0:T(8,128)} %get-tuple-element.13.gram_ref, f32[2,256,1024]{2,1,0:T(8,128)} %get-tuple-element.14.samples_ref), custom_call_target="tpu_custom_call" | custom-call | tf_op jit(solution)/shard_map/factor/pallas_call | solution.py:544
